TPU v7x, 32 devices: a whole 2x2x4 slice. The times are simulated.
32 devices in a mesh: slab: 4 (over x, core), energy: 8 (over z, y).
Axes of the slice: x: 2, y: 2, z: 4, core: 2. Of those that a mesh axis runs over, the one named last changes fastest.
Arguments:
- onsite: float32 [4, 384], P('slab'), may hold values from -1 to 1
- hopping: float32 [4, 384, 384], P('slab'), may hold values from -0.09 to 0.09, as said below
- separator_hamiltonian: float32 [128, 128], replicated, may hold values from -1 to 1, as said below
- coupling: float32 [4, 128], P('slab'), may hold values from 0.3 to 0.8
- bound_rows: int32 [4, 128], P('slab'), may hold values from 0 to 383, as said below
- old_sigma: float32 [2, 8, 4, 384, 384], P(None, 'energy', 'slab'), may hold values from -0.125 to 0.125
- phonon_vertex: float32 [4, 384, 384], P('slab'), may hold values from -0.3125 to 0.3125
- mode_steps: int32 [2], replicated, may hold values from 1 to 2, as said below
- mode_weights: float32 [2, 2], replicated, may hold values from 0.3 to 3
Outputs:
- new_sigma: float32 [2, 8, 4, 384, 384], P(None, 'energy', 'slab')
Inputs may be any that keep to these rules, and one draw needn't show every extreme that they name: Each slab's hopping block is symmetric with a zero diagonal. `separator_hamiltonian`: symmetric. `bound_rows`: each slab's 128 entries are distinct and ascending and include the slab's first and last orbital. `mode_steps`: the 2 modes have distinct steps.
All inputs are finite; a program needn't handle non-finite values.
Results may differ from a plain program's by a relative error of at most 0.0001.
Values sent between devices are 32-bit elements; how exact they have to be, the bound alone decides.
No kernel may reach another device: no remote copies, remote signals or barrier semaphores. Data moves between devices by JAX's collectives and lax.ppermute only.
A program may use at most 192 MiB of HBM per device.

v0:
```python
import functools

import jax
import jax.numpy as jnp
from jax import lax
from jax.experimental import pallas as pl
from jax.experimental.pallas import tpu as pltpu
from jax.sharding import PartitionSpec as P


BROADENING = 1.0
LOWEST = -2.0
SPREAD = 4.0

F32 = jnp.float32
BF16 = jnp.bfloat16
VMEM_BYTES = 24 << 20


def split(x):
    high = x.astype(BF16)
    return high, (x - high.astype(F32)).astype(BF16)


def turned(x):
    half = x.shape[1] // 2
    return jnp.concatenate([-x[:, half:], x[:, :half]], axis=1)


def left_of(x):
    high, low = split(x)
    return jnp.concatenate([high, high, low], axis=1)


def right_of(x):
    high, low = split(x)
    high = jnp.concatenate([high, turned(high)], axis=0)
    low = jnp.concatenate([low, turned(low)], axis=0)
    return jnp.concatenate([high, low, high], axis=0)


def dot(a, b):
    return jnp.dot(a, b, preferred_element_type=F32)


def product(a, b):
    return dot(left_of(a), right_of(b))


def row_scaled(factor, x):
    half = x.shape[1] // 2
    real, imag = x[:, :half], x[:, half:]
    return jnp.concatenate(
        [factor[0] * real - factor[1] * imag, factor[0] * imag + factor[1] * real], axis=1
    )


def same_place(shape):
    rows = lax.broadcasted_iota(jnp.int32, shape, 0)
    cols = lax.broadcasted_iota(jnp.int32, shape, 1)
    return rows == cols


def reciprocal(real, imag):
    magnitude = real * real + imag * imag
    return real / magnitude, -imag / magnitude


def reciprocal_diagonal(real, imag):
    tile = 128
    ways = ([], [])
    for at in range(0, real.shape[0], tile):
        blocks = [x[at : at + tile, at : at + tile] for x in (real, imag)]
        diagonal = same_place(blocks[0].shape)
        blocks = [jnp.where(diagonal, x, jnp.zeros_like(x)) for x in blocks]
        for axis in (0, 1):
            ways[axis].append([jnp.sum(x, axis=axis, keepdims=True) for x in blocks])
    across = [jnp.concatenate(part, axis=1) for part in zip(*ways[0])]
    down = [jnp.concatenate(part, axis=0) for part in zip(*ways[1])]
    return reciprocal(*across), reciprocal(*down)


def remainder(real, imag, across):
    diagonal = same_place(real.shape)
    zero = jnp.zeros_like(real)
    return jnp.concatenate(
        [
            jnp.where(diagonal, zero, imag * across[1] - real * across[0]),
            jnp.where(diagonal, zero, -(real * across[1]) - imag * across[0]),
        ],
        axis=1,
    )


def unit(shape):
    return jnp.where(same_place(shape), 1.0, 0.0)


def energy_here():
    index = lax.axis_index("energy")
    return LOWEST + SPREAD * (index.astype(F32) + 0.5) / lax.axis_size("energy")


def upright(x):
    size = x.shape[1]
    wide = jnp.broadcast_to(x, (size, size))
    return jnp.sum(jnp.where(same_place(wide.shape), wide, jnp.zeros_like(wide)), axis=1, keepdims=True)


def bound_kernel(*refs):
    sources, outs = refs[:5], refs[5:10]
    onsite, hopping, sigma, coupling, bound = places = refs[10:15]
    first_out, second_out, start_out, rows, term = outs
    arrived = refs[15]
    copies = [
        pltpu.make_async_copy(source, target, arrived.at[at])
        for at, (source, target) in enumerate(zip(sources, places))
    ]
    for copy in copies:
        copy.start()
    for copy in copies:
        copy.wait()
    size, few = hopping.shape[0], coupling.shape[1]
    diagonal = same_place(hopping.shape)
    level = energy_here() - onsite[...]
    real = jnp.where(diagonal, level, 0.0) - hopping[...] - sigma[0]
    imag = jnp.where(diagonal, BROADENING, 0.0) - sigma[1]
    across, down = reciprocal_diagonal(real, imag)
    first = remainder(real, imag, across)
    first_out[...] = first
    start_out[...] = jnp.concatenate(down, axis=1)
    second = product(first, first)
    second_out[...] = second
    places = bound[...]
    pick_rows = (
        lax.broadcasted_iota(jnp.int32, (few, size), 1) == upright(places.astype(F32)).astype(jnp.int32)
    ).astype(F32).astype(BF16)
    pick_cols = (lax.broadcasted_iota(jnp.int32, (size, few), 0) == places).astype(F32).astype(BF16)
    strength = coupling[...]
    high, low = split(row_scaled(down, unit(first.shape) + first))
    some = dot(pick_rows, high) + dot(pick_rows, low)
    right = right_of(second)
    some = some + dot(left_of(some), right)
    some = some + dot(left_of(dot(left_of(some), right)), right)
    some = some * upright(strength)
    rows[...] = some
    high, low = split(jnp.concatenate([some[:, :size], some[:, size:]], axis=0))
    corner = dot(high, pick_cols) + dot(low, pick_cols)
    corner = corner * strength
    term[...] = jnp.concatenate([corner[:few], corner[few:]], axis=1)


def power_kernel(first, second, start, partial, fourth):
    size = first.shape[0]
    one, two = first[...], second[...]
    both = dot(jnp.concatenate([left_of(one), left_of(two)], axis=0), right_of(two))
    total = unit(one.shape) + one + two + both[:size]
    partial[...] = row_scaled((start[:, 0:1], start[:, 1:2]), total)
    fourth[...] = both[size:]


def slab_kernel(partial, fourth, inverse):
    inverse[...] = partial[...] + product(partial[...], fourth[...])


def columns_of(x, places):
    size = x.shape[1] // 2
    pick = lax.broadcasted_iota(jnp.int32, (size, places.shape[1]), 0) == places
    pick = pick.astype(F32).astype(BF16)
    high, low = split(jnp.concatenate([x[:, :size], x[:, size:]], axis=0))
    chosen = dot(jnp.concatenate([high, low], axis=1), jnp.concatenate([pick, pick], axis=0))
    return jnp.concatenate([chosen[: x.shape[0]], chosen[x.shape[0] :]], axis=1)


def green_kernel(hamiltonian, coupling, bound, inverse, rows, near, far, middle, green_a, green_b):
    few = hamiltonian.shape[0]
    strength = coupling[...]
    columns = columns_of(inverse[...], bound[...]) * jnp.concatenate([strength, strength], axis=1)
    schur = near[...] + far[...]
    diagonal = same_place(hamiltonian.shape)
    real = jnp.where(diagonal, energy_here(), 0.0) - hamiltonian[...] - schur[:, :few]
    imag = jnp.where(diagonal, BROADENING, 0.0) - schur[:, few:]
    across, down = reciprocal_diagonal(real, imag)
    first = remainder(real, imag, across)
    second = product(first, first)
    both = dot(jnp.concatenate([left_of(first), left_of(second)], axis=0), right_of(second))
    total = row_scaled(down, unit(first.shape) + first + second + both[:few])
    separator = total + product(total, both[few:])
    inner = product(columns, separator)
    middle[...] = inner
    half, size = green_a.shape
    green = inverse[:, :size] + dot(left_of(inner), right_of(rows[...])[:, :size])
    green_a[...] = green[:half]
    green_b[...] = green[half:]


def imaginary_kernel(middle, rows, inverse, green_a, green_b):
    half, size = green_a.shape
    green = inverse[:, size:] + dot(left_of(middle[...]), right_of(rows[...])[:, size:])
    green_a[...] = green[:half]
    green_b[...] = green[half:]


def strengths(steps, weights):
    absorb, emit = [], []
    for distance in (1, 2):
        for row, out in ((0, absorb), (1, emit)):
            total = jnp.float32(0.0)
            for mode in range(steps.shape[0]):
                total = total + jnp.where(steps[mode] == distance, weights[row, mode], 0.0)
            out.append(total)
    return absorb, emit


def place():
    energy, count = lax.axis_index("energy"), lax.axis_size("energy")
    odd = lax.rem(energy, 2) == 1
    odd_pair = lax.rem(lax.div(energy, 2), 2) == 1
    lower, higher = energy >= 2, energy + 2 < count
    one = jnp.where(odd_pair, lower.astype(jnp.int32), higher.astype(jnp.int32)) == 1
    two = jnp.where(odd_pair, higher.astype(jnp.int32), lower.astype(jnp.int32)) == 1
    return odd, odd_pair, one, two


def kept(there, x):
    return jnp.where(there, x, jnp.zeros_like(x))


def combine_kernel(steps, weights, green_a, green_b, one_a, two_a, pair_b, across_a, one_b, two_b):
    absorb, emit = strengths(steps, weights)
    odd, odd_pair, one, two = place()
    zero = jnp.float32(0.0)
    from_one = jnp.where(odd, jnp.where(odd_pair, absorb[0], zero), jnp.where(odd_pair, zero, emit[0]))
    from_two = jnp.where(odd, jnp.where(odd_pair, zero, absorb[0]), jnp.where(odd_pair, emit[0], zero))
    across_a[...] = (
        jnp.where(odd, emit[0], absorb[0]) * green_a[...]
        + from_one * kept(one, one_a[...])
        + from_two * kept(two, two_a[...])
    )
    up = (absorb[1], jnp.where(odd, zero, absorb[0]))
    down = (emit[1], jnp.where(odd, emit[0], zero))
    for out, first, second in ((one_b, up, down), (two_b, down, up)):
        own, other = [jnp.where(odd_pair, b, a) for a, b in zip(first, second)]
        out[...] = own * green_b[...] + other * pair_b[...]


def dressed(left, right, mixed):
    high, low = split(mixed)
    outer = dot(jnp.concatenate([high, high, low], axis=1), right[...])
    high, low = split(outer)
    return dot(left[...], jnp.concatenate([high, low, high], axis=0))


def dress_a_kernel(steps, weights, left, right, one_a, two_a, across_a, out):
    absorb, emit = strengths(steps, weights)
    _, odd_pair, one, two = place()
    from_one = jnp.where(odd_pair, absorb[1], emit[1])
    from_two = jnp.where(odd_pair, emit[1], absorb[1])
    mixed = from_one * kept(one, one_a[...]) + from_two * kept(two, two_a[...]) + across_a[...]
    out[...] = dressed(left, right, mixed)


def dress_b_kernel(steps, weights, left, right, one_b, two_b, pair_b, other, *rest):
    absorb, emit = strengths(steps, weights)
    odd, _, one, two = place()
    mixed = kept(one, one_b[...]) + kept(two, two_b[...]) + jnp.where(odd, absorb[0], emit[0]) * pair_b[...]
    out = rest[-1]
    out[0] = other[...] + dressed(left, right, mixed)


def vertex_left_kernel(vertex, left_a, left_b):
    half = left_a.shape[1] // 3
    high, low = split(vertex[...])
    for side, left in enumerate((left_a, left_b)):
        part = (slice(None), slice(side * half, side * half + half))
        left[...] = jnp.concatenate([high[part], high[part], low[part]], axis=1)


def vertex_right_kernel(vertex, right):
    size = vertex.shape[0]
    high, low = split(vertex[...].T)
    for at, part in enumerate((high, low, high)):
        right[at * size : (at + 1) * size, :] = part


def call(kernel, outs, args, scalars=0, flops=0, **kept):
    vmem = pl.BlockSpec(memory_space=pltpu.VMEM)
    smem = pl.BlockSpec(memory_space=pltpu.SMEM)
    touched = sum(4 * a.size for a in [*args, *jax.tree.leaves(outs)])
    settings = dict(
        in_specs=[smem] * scalars + [vmem] * (len(args) - scalars),
        out_specs=jax.tree.map(lambda _: vmem, outs),
    )
    settings.update(kept)
    return pl.pallas_call(
        kernel,
        out_shape=outs,
        compiler_params=pltpu.CompilerParams(vmem_limit_bytes=VMEM_BYTES),
        cost_estimate=pl.CostEstimate(flops=flops, bytes_accessed=touched, transcendentals=0),
        **settings,
    )(*args)


def held(*shape):
    return jax.ShapeDtypeStruct(shape, F32)


def exchange(x, partner):
    slabs, energies = lax.axis_size("slab"), lax.axis_size("energy")
    pairs = []
    for slab in range(slabs):
        for energy in range(energies):
            other = partner(energy)
            if 0 <= other < energies:
                target = slab * energies + other
            else:
                target = (slab ^ 1) % slabs * energies + energy
            pairs.append((slab * energies + energy, target))
    return lax.ppermute(x, ("slab", "energy"), pairs)


def in_pair(energy):
    return energy ^ 1


def in_one(energy):
    return energy ^ 2


def in_two(energy):
    return energy + 2 if energy // 2 % 2 == 1 else energy - 2


def per_device(
    onsite,
    hopping,
    separator_hamiltonian,
    coupling,
    bound_rows,
    old_sigma,
    phonon_vertex,
    mode_steps,
    mode_weights,
):
    size, few = hopping.shape[-1], coupling.shape[-1]
    energies, slabs = lax.axis_size("energy"), lax.axis_size("slab")
    assert energies % 2 == 0 and slabs & (slabs - 1) == 0
    half = size // 2
    cube = 3 * 8 * size**3
    full = held(size, 2 * size)
    sigma = old_sigma.reshape(2, size, size)
    given = [
        pltpu.with_memory_space_constraint(x, pltpu.HBM)
        for x in (onsite, hopping[0], sigma, coupling, bound_rows)
    ]
    first, second, start, rows, term = call(
        bound_kernel,
        [full, full, held(size, 2), held(few, 2 * size), held(few, 2 * few)],
        given,
        flops=2 * cube,
        in_specs=[pl.BlockSpec(memory_space=pltpu.HBM)] * len(given),
        scratch_shapes=[pltpu.VMEM(x.shape, x.dtype) for x in given]
        + [pltpu.SemaphoreType.DMA((len(given),))],
    )
    partial, fourth = call(power_kernel, [full, full], [first, second, start], flops=2 * cube)
    near, far, reach = term, None, slabs // 2
    while reach:
        if far is not None:
            far, fourth = lax.optimization_barrier((far, fourth))
            near = near + far
        far = lax.ppermute(near, "slab", [(i, i ^ reach) for i in range(slabs)])
        reach //= 2
    inverse = call(slab_kernel, full, [partial, fourth], flops=cube)
    part = held(half, size)
    middle, *greens = call(
        green_kernel,
        [held(size, 2 * few), part, part],
        [separator_hamiltonian, coupling, bound_rows, inverse, rows, near, far],
        flops=cube,
    )
    parts = []
    for at in (0, 1):
        green_a, green_b = greens
        two_a = exchange(green_a, in_two)
        one_a = exchange(green_a, in_one)
        pair_b = exchange(green_b, in_pair)
        parts.append((green_a, green_b, one_a, two_a, pair_b))
        if at == 0:
            greens = call(imaginary_kernel, [part, part], [middle, rows, inverse], flops=cube // 4)
    combined = []
    for part in parts:
        across_a, one_b, two_b = call(
            combine_kernel, [held(half, size)] * 3, [mode_steps, mode_weights, *part], scalars=2
        )
        two_b = exchange(two_b, in_two)
        one_b = exchange(one_b, in_one)
        across_a = exchange(across_a, in_pair)
        combined.append((across_a, one_b, two_b))
    lefts = jax.ShapeDtypeStruct((size, 3 * half), BF16)
    left_a, left_b = call(vertex_left_kernel, [lefts, lefts], [phonon_vertex[0]])
    right = call(
        vertex_right_kernel, jax.ShapeDtypeStruct((3 * size, size), BF16), [phonon_vertex[0]]
    )
    out = None
    for at, (part, more) in enumerate(zip(parts, combined)):
        _, _, one_a, two_a, pair_b = part
        across_a, one_b, two_b = more
        other = call(
            dress_a_kernel,
            held(size, size),
            [mode_steps, mode_weights, left_a, right, one_a, two_a, across_a],
            scalars=2,
            flops=cube // 8,
        )
        args = [mode_steps, mode_weights, left_b, right, one_b, two_b, pair_b, other]
        vmem = pl.BlockSpec(memory_space=pltpu.VMEM)
        specs = [pl.BlockSpec(memory_space=pltpu.SMEM)] * 2 + [vmem] * (len(args) - 2)
        aliases = {}
        if out is not None:
            aliases = {len(args): 0}
            args, specs = [*args, out], [*specs, pl.BlockSpec(memory_space=pl.ANY)]
        out = call(
            dress_b_kernel,
            held(2, size, size),
            args,
            flops=cube // 8,
            in_specs=specs,
            grid=(1,),
            out_specs=pl.BlockSpec((1, size, size), functools.partial(lambda at, i: (at, 0, 0), at)),
            input_output_aliases=aliases,
        )
    return out.reshape(old_sigma.shape)


def solution(mesh):
    placed = (
        P("slab", None),
        P("slab", None, None),
        P(),
        P("slab", None),
        P("slab", None),
        P(None, "energy", "slab", None, None),
        P("slab", None, None),
        P(),
        P(),
    )

    return jax.shard_map(
        per_device,
        mesh=mesh,
        in_specs=placed,
        out_specs=P(None, "energy", "slab", None, None),
        check_vma=False,
    )
```

profile of v0, /device:TPU:0, one launch (start us, length us, event | category | flops | bytes accessed | tf_op | source)
XLA Modules:
  0.0 53.5 jit_solution(1701222721771391081)
XLA Ops:
  0.0 6.1 %shard_map.93 = (f32[384,768]{1,0:T(8,128)S(1)}, f32[384,768]{1,0:T(8,128)S(1)}, f32[384,2]{1,0:T(8,128)S(1)}, f32[128,768]{1,0:T(8,128)S(1)}, f32[128,256]{1,0:T(8,128)S(1)}) custom-call(f32[1,384]{1,0:T(1,128)} %refs_0_.1, f32[384,384]{1,0:T(8,128)} %bitcast.9, f32[2,384,384]{2,1,0:T(8,128)} %bitcast.8, f32[1,128]{1,0:T(1,128)} %coupling.1, s32[1,128]{1,0:T(1,128)} %bound.1), custom_call_target="tpu_custom_call" | custom-call | flops 2717908992 | bytes 4658688 | tf_op jit(solution)/shard_map/pallas_call | solution.py:295
  6.1 3.0 %collective-permute-start = (f32[128,256]{1,0:T(8,128)S(1)}, f32[128,256]{1,0:T(8,128)S(1)}, u32[]{:S(2)}, u32[]{:S(2)}) collective-permute-start(f32[128,256]{1,0:T(8,128)S(1)} %get-tuple-element.32), channel_id=1, source_target_pairs={{0,16},{8,24},{16,0},{24,8},{1,17},{9,25},{17,1},{25,9},{2,18},{10... | collective-permute-start | bytes 393224 | tf_op jit(solution)/shard_map/ppermute | solution.py:371
  9.2 3.0 %shard_map.94 = (f32[384,768]{1,0:T(8,128)S(1)}, f32[384,768]{1,0:T(8,128)S(1)}) custom-call(f32[384,768]{1,0:T(8,128)S(1)} %get-tuple-element.28.first, f32[384,768]{1,0:T(8,128)S(1)} %get-tuple-element.29.second, f32[384,2]{1,0:T(8,128)S(1)} %get-tuple-element.30.start), custom_call_target="tpu_custom_call" | custom-call | flops 2717908992 | bytes 4721664 | tf_op jit(solution)/shard_map/pallas_call | solution.py:295
  12.2 0.5 collective-permute-done
  12.7 0.1 collective-permute-start.1
  12.8 0.0 copy-start.3
  12.8 0.0 copy-start.4
  12.8 0.0 copy-start.5
  12.8 1.6 %shard_map.95.inverse = f32[384,768]{1,0:T(8,128)S(1)} custom-call(f32[384,768]{1,0:T(8,128)S(1)} %get-tuple-element.31.partial, f32[384,768]{1,0:T(8,128)S(1)} %get-tuple-element.34.fourth), custom_call_target="tpu_custom_call" | custom-call | flops 1358954496 | bytes 3538944 | tf_op jit(solution)/shard_map/pallas_call | solution.py:295
  14.4 0.0 collective-permute-done.1.far
  14.4 0.0 copy-done.3
  14.4 1.8 %shard_map.96 = (f32[384,256]{1,0:T(8,128)S(1)}, f32[192,384]{1,0:T(8,128)S(1)}, f32[192,384]{1,0:T(8,128)S(1)}) custom-call(f32[128,128]{1,0:T(8,128)S(1)} %copy-done.3, f32[1,128]{1,0:T(1,128)S(1)} %copy-done.4, s32[1,128]{1,0:T(1,128)S(1)} %copy-done.5, f32[384,768]{1,0:T(8,128)S(1)} %shard_map.95.inverse, f32[128,768]{1,0:T(8,128)S(1)} %get-tuple-element.35.rows, ...), custom_call_target="tpu_custom_call" | custom-call | flops 1358954496 | bytes 2884608 | tf_op jit(solution)/shard_map/pallas_call | solution.py:295
  16.3 0.0 copy-start.1
  16.3 0.0 copy-start.2
  16.3 1.8 %collective-permute-start.10 = (f32[192,384]{1,0:T(8,128)S(1)}, f32[192,384]{1,0:T(8,128)S(1)}, u32[]{:S(2)}, u32[]{:S(2)}) collective-permute-start(f32[192,384]{1,0:T(8,128)S(1)} %get-tuple-element.45.green_b), channel_id=1, source_target_pairs={{0,1},{1,0},{2,3},{3,2},{4,5},{5,4},{6,7},{7,6},{8,9},{9,8},{10,11... | collective-permute-start | bytes 884744 | tf_op jit(solution)/shard_map/ppermute | solution.py:319
  18.1 1.6 %collective-permute-start.8 = (f32[192,384]{1,0:T(8,128)S(1)}, f32[192,384]{1,0:T(8,128)S(1)}, u32[]{:S(2)}, u32[]{:S(2)}) collective-permute-start(f32[192,384]{1,0:T(8,128)S(1)} %get-tuple-element.44.green_a), channel_id=1, source_target_pairs={{0,2},{1,3},{2,0},{3,1},{4,6},{5,7},{6,4},{7,5},{8,10},{9,11},{10,... | collective-permute-start | bytes 884744 | tf_op jit(solution)/shard_map/ppermute | solution.py:319
  19.7 0.0 collective-permute-start.9
  19.7 0.5 shard_map.97
  20.2 3.2 %collective-permute-start.2 = (f32[192,384]{1,0:T(8,128)S(1)}, f32[192,384]{1,0:T(8,128)S(1)}, u32[]{:S(2)}, u32[]{:S(2)}) collective-permute-start(f32[192,384]{1,0:T(8,128)S(1)} %get-tuple-element.38.green_a), channel_id=1, source_target_pairs={{0,2},{1,3},{2,0},{3,1},{4,6},{5,7},{6,4},{7,5},{8,10},{9,11},{10,... | collective-permute-start | bytes 884744 | tf_op jit(solution)/shard_map/ppermute | solution.py:319
  23.4 0.0 collective-permute-start.3
  23.4 2.4 %collective-permute-done.10.pair_b = f32[192,384]{1,0:T(8,128)S(1)} collective-permute-done((f32[192,384]{1,0:T(8,128)S(1)}, f32[192,384]{1,0:T(8,128)S(1)}, u32[]{:S(2)}, u32[]{:S(2)}) %collective-permute-start.10) | collective-permute-done | bytes 294944 | tf_op jit(solution)/shard_map/ppermute | solution.py:319
  25.8 1.7 %collective-permute-start.4 = (f32[192,384]{1,0:T(8,128)S(1)}, f32[192,384]{1,0:T(8,128)S(1)}, u32[]{:S(2)}, u32[]{:S(2)}) collective-permute-start(f32[192,384]{1,0:T(8,128)S(1)} %get-tuple-element.39.green_b), channel_id=1, source_target_pairs={{0,1},{1,0},{2,3},{3,2},{4,5},{5,4},{6,7},{7,6},{8,9},{9,8},{10,11... | collective-permute-start | bytes 884744 | tf_op jit(solution)/shard_map/ppermute | solution.py:319
  27.5 0.5 collective-permute-done.8.one_a
  28.0 0.0 collective-permute-done.9.two_a
  28.0 0.7 %shard_map.100 = (f32[192,384]{1,0:T(8,128)S(1)}, f32[192,384]{1,0:T(8,128)S(1)}, f32[192,384]{1,0:T(8,128)S(1)}) custom-call(s32[2]{0:T(128)S(1)} %copy-done.2, f32[2,2]{1,0:T(2,128)S(1)} %copy-done.1, f32[192,384]{1,0:T(8,128)S(1)} %get-tuple-element.44.green_a, f32[192,384]{1,0:T(8,128)S(1)} %get-tuple-element.45.green_b, ...), custom_call_target="tpu_custom_call" | custom-call | bytes 2359320 | tf_op jit(solution)/shard_map/pallas_call | solution.py:295
  28.7 0.3 collective-permute-start.13
  29.1 4.5 %collective-permute-done.2.one_a = f32[192,384]{1,0:T(8,128)S(1)} collective-permute-done((f32[192,384]{1,0:T(8,128)S(1)}, f32[192,384]{1,0:T(8,128)S(1)}, u32[]{:S(2)}, u32[]{:S(2)}) %collective-permute-start.2) | collective-permute-done | bytes 294944 | tf_op jit(solution)/shard_map/ppermute | solution.py:319
  33.6 0.0 collective-permute-done.3.two_a
  33.6 2.1 %collective-permute-done.4.pair_b = f32[192,384]{1,0:T(8,128)S(1)} collective-permute-done((f32[192,384]{1,0:T(8,128)S(1)}, f32[192,384]{1,0:T(8,128)S(1)}, u32[]{:S(2)}, u32[]{:S(2)}) %collective-permute-start.4) | collective-permute-done | bytes 294944 | tf_op jit(solution)/shard_map/ppermute | solution.py:319
  35.7 0.7 %shard_map.98 = (f32[192,384]{1,0:T(8,128)S(1)}, f32[192,384]{1,0:T(8,128)S(1)}, f32[192,384]{1,0:T(8,128)S(1)}) custom-call(s32[2]{0:T(128)S(1)} %copy-done.2, f32[2,2]{1,0:T(2,128)S(1)} %copy-done.1, f32[192,384]{1,0:T(8,128)S(1)} %get-tuple-element.38.green_a, f32[192,384]{1,0:T(8,128)S(1)} %get-tuple-element.39.green_b, ...), custom_call_target="tpu_custom_call" | custom-call | bytes 2359320 | tf_op jit(solution)/shard_map/pallas_call | solution.py:295
  36.4 1.8 %collective-permute-start.7 = (f32[192,384]{1,0:T(8,128)S(1)}, f32[192,384]{1,0:T(8,128)S(1)}, u32[]{:S(2)}, u32[]{:S(2)}) collective-permute-start(f32[192,384]{1,0:T(8,128)S(1)} %get-tuple-element.43), channel_id=1, source_target_pairs={{0,1},{1,0},{2,3},{3,2},{4,5},{5,4},{6,7},{7,6},{8,9},{9,8},{10,11... | collective-permute-start | bytes 884744 | tf_op jit(solution)/shard_map/ppermute | solution.py:319
  38.2 1.6 %collective-permute-start.11 = (f32[192,384]{1,0:T(8,128)S(1)}, f32[192,384]{1,0:T(8,128)S(1)}, u32[]{:S(2)}, u32[]{:S(2)}) collective-permute-start(f32[192,384]{1,0:T(8,128)S(1)} %get-tuple-element.46), channel_id=1, source_target_pairs={{0,2},{1,3},{2,0},{3,1},{4,6},{5,7},{6,4},{7,5},{8,10},{9,11},{10,... | collective-permute-start | bytes 884744 | tf_op jit(solution)/shard_map/ppermute | solution.py:319
  39.8 0.0 collective-permute-start.12
  39.8 3.1 %collective-permute-start.5 = (f32[192,384]{1,0:T(8,128)S(1)}, f32[192,384]{1,0:T(8,128)S(1)}, u32[]{:S(2)}, u32[]{:S(2)}) collective-permute-start(f32[192,384]{1,0:T(8,128)S(1)} %get-tuple-element.40), channel_id=1, source_target_pairs={{0,2},{1,3},{2,0},{3,1},{4,6},{5,7},{6,4},{7,5},{8,10},{9,11},{10,... | collective-permute-start | bytes 884744 | tf_op jit(solution)/shard_map/ppermute | solution.py:319
  42.9 0.0 collective-permute-done.13.across_a
  42.9 0.0 collective-permute-start.6
  42.9 0.0 copy-done
  42.9 0.2 shard_map.92.right
  43.2 0.2 shard_map.91
  43.4 1.4 %shard_map.101.other = f32[384,384]{1,0:T(8,128)S(1)} custom-call(s32[2]{0:T(128)S(1)} %copy-done.2, f32[2,2]{1,0:T(2,128)S(1)} %copy-done.1, bf16[384,576]{1,0:T(8,128)(2,1)S(1)} %get-tuple-element.42.left, bf16[1152,384]{1,0:T(8,128)(2,1)S(1)} %shard_map.92.right, f32[192,384]{1,0:T(8,128)S(1)} %collective-permute-done.8.one_a, ...), custom_call_target="tpu_custom_call" | custom-call | flops 169869312 | bytes 4128792 | tf_op jit(solution)/shard_map/pallas_call | solution.py:295
  44.8 2.2 %collective-permute-done.7.across_a = f32[192,384]{1,0:T(8,128)S(1)} collective-permute-done((f32[192,384]{1,0:T(8,128)S(1)}, f32[192,384]{1,0:T(8,128)S(1)}, u32[]{:S(2)}, u32[]{:S(2)}) %collective-permute-start.7) | collective-permute-done | bytes 294944 | tf_op jit(solution)/shard_map/ppermute | solution.py:319
  47.0 1.4 %shard_map.99.other = f32[384,384]{1,0:T(8,128)S(1)} custom-call(s32[2]{0:T(128)S(1)} %copy-done.2, f32[2,2]{1,0:T(2,128)S(1)} %copy-done.1, bf16[384,576]{1,0:T(8,128)(2,1)S(1)} %get-tuple-element.42.left, bf16[1152,384]{1,0:T(8,128)(2,1)S(1)} %shard_map.92.right, f32[192,384]{1,0:T(8,128)S(1)} %collective-permute-done.2.one_a, ...), custom_call_target="tpu_custom_call" | custom-call | flops 169869312 | bytes 4128792 | tf_op jit(solution)/shard_map/pallas_call | solution.py:295
  48.4 0.0 collective-permute-done.11.one_b
  48.4 0.0 collective-permute-done.12.two_b
  48.4 2.3 %shard_map.102.rest_0_ = f32[2,384,384]{2,1,0:T(8,128)} custom-call(s32[2]{0:T(128)S(1)} %copy-done.2, f32[2,2]{1,0:T(2,128)S(1)} %copy-done.1, bf16[384,576]{1,0:T(8,128)(2,1)S(1)} %get-tuple-element.27.left, bf16[1152,384]{1,0:T(8,128)(2,1)S(1)} %shard_map.92.right, f32[192,384]{1,0:T(8,128)S(1)} %collective-permute-done.11.one_b, ...), custom_call_target="tpu_custom_call" | custom-call | flops 169869312 | bytes 5308440 | tf_op jit(solution)/shard_map/pallas_call | solution.py:295
  50.7 0.6 %collective-permute-done.5.one_b = f32[192,384]{1,0:T(8,128)S(1)} collective-permute-done((f32[192,384]{1,0:T(8,128)S(1)}, f32[192,384]{1,0:T(8,128)S(1)}, u32[]{:S(2)}, u32[]{:S(2)}) %collective-permute-start.5) | collective-permute-done | bytes 294944 | tf_op jit(solution)/shard_map/ppermute | solution.py:319
  51.2 0.0 collective-permute-done.6.two_b
  51.2 2.2 %shard_map.103 = f32[2,384,384]{2,1,0:T(8,128)} custom-call(s32[2]{0:T(128)S(1)} %copy-done.2, f32[2,2]{1,0:T(2,128)S(1)} %copy-done.1, bf16[384,576]{1,0:T(8,128)(2,1)S(1)} %get-tuple-element.27.left, bf16[1152,384]{1,0:T(8,128)(2,1)S(1)} %shard_map.92.right, f32[192,384]{1,0:T(8,128)S(1)} %collective-permute-done.5.one_b, ...), custom_call_target="tpu_custom_call", output_to_operand_aliasing={{}: (8, {})} | custom-call | flops 169869312 | bytes 6488088 | tf_op jit(solution)/shard_map/pallas_call | solution.py:295
  (6 shorter events, 0.0 us)
Async XLA Ops:
  6.1 6.5 %collective-permute-start = (f32[128,256]{1,0:T(8,128)S(1)}, f32[128,256]{1,0:T(8,128)S(1)}, u32[]{:S(2)}, u32[]{:S(2)}) collective-permute-start(f32[128,256]{1,0:T(8,128)S(1)} %get-tuple-element.32), channel_id=1, source_target_pairs={{0,16},{8,24},{16,0},{24,8},{1,17},{9,25},{17,1},{25,9},{2,18},{10... | collective-permute-start | bytes 393224 | tf_op jit(solution)/shard_map/ppermute | solution.py:371
  12.7 1.7 %collective-permute-start.1 = (f32[128,256]{1,0:T(8,128)S(1)}, f32[128,256]{1,0:T(8,128)S(1)}, u32[]{:S(2)}, u32[]{:S(2)}) collective-permute-start(f32[128,256]{1,0:T(8,128)S(1)} %add.3.near), channel_id=1, source_target_pairs={{0,8},{8,0},{16,24},{24,16},{1,9},{9,1},{17,25},{25,17},{2,10},{10... | collective-permute-start | bytes 393224 | tf_op jit(solution)/shard_map/ppermute | solution.py:371
  12.8 1.6 %copy-start.3 = (f32[128,128]{1,0:T(8,128)S(1)}, f32[128,128]{1,0:T(8,128)}, u32[]{:S(2)}) copy-start(f32[128,128]{1,0:T(8,128)} %hamiltonian.1) | copy-start | bytes 196612
  12.8 1.6 %copy-start.4 = (f32[1,128]{1,0:T(1,128)S(1)}, f32[1,128]{1,0:T(1,128)}, u32[]{:S(2)}) copy-start(f32[1,128]{1,0:T(1,128)} %coupling.1) | copy-start | bytes 1540
  12.8 1.6 %copy-start.5 = (s32[1,128]{1,0:T(1,128)S(1)}, s32[1,128]{1,0:T(1,128)}, u32[]{:S(2)}) copy-start(s32[1,128]{1,0:T(1,128)} %bound.1) | copy-start | bytes 1540
  16.3 11.7 %copy-start.1 = (f32[2,2]{1,0:T(2,128)S(1)}, f32[2,2]{1,0:T(2,128)}, u32[]{:S(2)}) copy-start(f32[2,2]{1,0:T(2,128)} %weights.11) | copy-start | bytes 52
  16.3 11.7 %copy-start.2 = (s32[2]{0:T(128)S(1)}, s32[2]{0:T(128)}, u32[]{:S(2)}) copy-start(s32[2]{0:T(128)} %steps.11) | copy-start | bytes 28
  16.3 9.5 %collective-permute-start.10 = (f32[192,384]{1,0:T(8,128)S(1)}, f32[192,384]{1,0:T(8,128)S(1)}, u32[]{:S(2)}, u32[]{:S(2)}) collective-permute-start(f32[192,384]{1,0:T(8,128)S(1)} %get-tuple-element.45.green_b), channel_id=1, source_target_pairs={{0,1},{1,0},{2,3},{3,2},{4,5},{5,4},{6,7},{7,6},{8,9},{9,8},{10,11... | collective-permute-start | bytes 884744 | tf_op jit(solution)/shard_map/ppermute | solution.py:319
  18.1 9.9 %collective-permute-start.8 = (f32[192,384]{1,0:T(8,128)S(1)}, f32[192,384]{1,0:T(8,128)S(1)}, u32[]{:S(2)}, u32[]{:S(2)}) collective-permute-start(f32[192,384]{1,0:T(8,128)S(1)} %get-tuple-element.44.green_a), channel_id=1, source_target_pairs={{0,2},{1,3},{2,0},{3,1},{4,6},{5,7},{6,4},{7,5},{8,10},{9,11},{10,... | collective-permute-start | bytes 884744 | tf_op jit(solution)/shard_map/ppermute | solution.py:319
  19.7 8.3 %collective-permute-start.9 = (f32[192,384]{1,0:T(8,128)S(1)}, f32[192,384]{1,0:T(8,128)S(1)}, u32[]{:S(2)}, u32[]{:S(2)}) collective-permute-start(f32[192,384]{1,0:T(8,128)S(1)} %get-tuple-element.44.green_a), channel_id=1, source_target_pairs={{0,8},{1,9},{2,4},{3,5},{4,2},{5,3},{6,14},{7,15},{8,0},{9,1},{10,... | collective-permute-start | bytes 884744 | tf_op jit(solution)/shard_map/ppermute | solution.py:319
  20.2 13.4 %collective-permute-start.2 = (f32[192,384]{1,0:T(8,128)S(1)}, f32[192,384]{1,0:T(8,128)S(1)}, u32[]{:S(2)}, u32[]{:S(2)}) collective-permute-start(f32[192,384]{1,0:T(8,128)S(1)} %get-tuple-element.38.green_a), channel_id=1, source_target_pairs={{0,2},{1,3},{2,0},{3,1},{4,6},{5,7},{6,4},{7,5},{8,10},{9,11},{10,... | collective-permute-start | bytes 884744 | tf_op jit(solution)/shard_map/ppermute | solution.py:319
  23.4 10.1 %collective-permute-start.3 = (f32[192,384]{1,0:T(8,128)S(1)}, f32[192,384]{1,0:T(8,128)S(1)}, u32[]{:S(2)}, u32[]{:S(2)}) collective-permute-start(f32[192,384]{1,0:T(8,128)S(1)} %get-tuple-element.38.green_a), channel_id=1, source_target_pairs={{0,8},{1,9},{2,4},{3,5},{4,2},{5,3},{6,14},{7,15},{8,0},{9,1},{10,... | collective-permute-start | bytes 884744 | tf_op jit(solution)/shard_map/ppermute | solution.py:319
  25.8 17.1 %copy-start = (f32[1,384,384]{2,1,0:T(8,128)S(1)}, f32[1,384,384]{2,1,0:T(8,128)}, u32[]{:S(2)}) copy-start(f32[1,384,384]{2,1,0:T(8,128)} %param.15) | copy-start | bytes 1769476
  25.8 9.9 %collective-permute-start.4 = (f32[192,384]{1,0:T(8,128)S(1)}, f32[192,384]{1,0:T(8,128)S(1)}, u32[]{:S(2)}, u32[]{:S(2)}) collective-permute-start(f32[192,384]{1,0:T(8,128)S(1)} %get-tuple-element.39.green_b), channel_id=1, source_target_pairs={{0,1},{1,0},{2,3},{3,2},{4,5},{5,4},{6,7},{7,6},{8,9},{9,8},{10,11... | collective-permute-start | bytes 884744 | tf_op jit(solution)/shard_map/ppermute | solution.py:319
  28.7 14.2 %collective-permute-start.13 = (f32[192,384]{1,0:T(8,128)S(1)}, f32[192,384]{1,0:T(8,128)S(1)}, u32[]{:S(2)}, u32[]{:S(2)}) collective-permute-start(f32[192,384]{1,0:T(8,128)S(1)} %get-tuple-element.48), channel_id=1, source_target_pairs={{0,1},{1,0},{2,3},{3,2},{4,5},{5,4},{6,7},{7,6},{8,9},{9,8},{10,11... | collective-permute-start | bytes 884744 | tf_op jit(solution)/shard_map/ppermute | solution.py:319
  36.4 10.6 %collective-permute-start.7 = (f32[192,384]{1,0:T(8,128)S(1)}, f32[192,384]{1,0:T(8,128)S(1)}, u32[]{:S(2)}, u32[]{:S(2)}) collective-permute-start(f32[192,384]{1,0:T(8,128)S(1)} %get-tuple-element.43), channel_id=1, source_target_pairs={{0,1},{1,0},{2,3},{3,2},{4,5},{5,4},{6,7},{7,6},{8,9},{9,8},{10,11... | collective-permute-start | bytes 884744 | tf_op jit(solution)/shard_map/ppermute | solution.py:319
  38.2 10.2 %collective-permute-start.11 = (f32[192,384]{1,0:T(8,128)S(1)}, f32[192,384]{1,0:T(8,128)S(1)}, u32[]{:S(2)}, u32[]{:S(2)}) collective-permute-start(f32[192,384]{1,0:T(8,128)S(1)} %get-tuple-element.46), channel_id=1, source_target_pairs={{0,2},{1,3},{2,0},{3,1},{4,6},{5,7},{6,4},{7,5},{8,10},{9,11},{10,... | collective-permute-start | bytes 884744 | tf_op jit(solution)/shard_map/ppermute | solution.py:319
  39.8 8.6 %collective-permute-start.12 = (f32[192,384]{1,0:T(8,128)S(1)}, f32[192,384]{1,0:T(8,128)S(1)}, u32[]{:S(2)}, u32[]{:S(2)}) collective-permute-start(f32[192,384]{1,0:T(8,128)S(1)} %get-tuple-element.47), channel_id=1, source_target_pairs={{0,8},{1,9},{2,4},{3,5},{4,2},{5,3},{6,14},{7,15},{8,0},{9,1},{10,... | collective-permute-start | bytes 884744 | tf_op jit(solution)/shard_map/ppermute | solution.py:319
  39.8 11.4 %collective-permute-start.5 = (f32[192,384]{1,0:T(8,128)S(1)}, f32[192,384]{1,0:T(8,128)S(1)}, u32[]{:S(2)}, u32[]{:S(2)}) collective-permute-start(f32[192,384]{1,0:T(8,128)S(1)} %get-tuple-element.40), channel_id=1, source_target_pairs={{0,2},{1,3},{2,0},{3,1},{4,6},{5,7},{6,4},{7,5},{8,10},{9,11},{10,... | collective-permute-start | bytes 884744 | tf_op jit(solution)/shard_map/ppermute | solution.py:319
  42.9 8.3 %collective-permute-start.6 = (f32[192,384]{1,0:T(8,128)S(1)}, f32[192,384]{1,0:T(8,128)S(1)}, u32[]{:S(2)}, u32[]{:S(2)}) collective-permute-start(f32[192,384]{1,0:T(8,128)S(1)} %get-tuple-element.41), channel_id=1, source_target_pairs={{0,8},{1,9},{2,4},{3,5},{4,2},{5,3},{6,14},{7,15},{8,0},{9,1},{10,... | collective-permute-start | bytes 884744 | tf_op jit(solution)/shard_map/ppermute | solution.py:319
where the time goes:
time: 53.6 us; the launch traced here: 53.5 us
  Pallas kernels  22.2 us (41%)
  starting transfers between devices  18.3 us (34%)
  waiting for transfers between devices  12.7 us (24%)
    pallas_call x13, Pallas kernels, call(): pl.pallas_call(kernel, out_shape=outs, compiler_params=pltpu.CompilerPara...  22.2 us
    ppermute x12, starting transfers between devices, exchange(): return lax.ppermute(x, ('slab', 'energy'), pairs)  15.2 us
    ppermute x12, waiting for transfers between devices, exchange(): return lax.ppermute(x, ('slab', 'energy'), pairs)  12.2 us
    ppermute x2, starting transfers between devices, per_device(): far = lax.ppermute(near, 'slab', [(i, i ^ reach) for i in range(slabs)])  3.11 us
  transfers between devices with their start and end apart: 14, of which 7 were waited for; matrix products, arithmetic and copies ran while one was open for 0% of the time, Pallas kernels for 22%

commit v1 on v0

--- a/solution.py
+++ b/solution.py
@@ -244,36 +244,33 @@
         out[...] = own * green_b[...] + other * pair_b[...]
 
 
-def dressed(left, right, mixed):
-    high, low = split(mixed)
-    outer = dot(jnp.concatenate([high, high, low], axis=1), right[...])
-    high, low = split(outer)
-    return dot(left[...], jnp.concatenate([high, low, high], axis=0))
-
-
-def dress_a_kernel(steps, weights, left, right, one_a, two_a, across_a, out):
+def dress_kernel(at, steps, weights, left, right, one_a, two_a, across_a, one_b, two_b, pair_b, *rest):
+    out, held_out, sent = rest[-3:]
     absorb, emit = strengths(steps, weights)
-    _, odd_pair, one, two = place()
+    odd, odd_pair, one, two = place()
     from_one = jnp.where(odd_pair, absorb[1], emit[1])
     from_two = jnp.where(odd_pair, emit[1], absorb[1])
-    mixed = from_one * kept(one, one_a[...]) + from_two * kept(two, two_a[...]) + across_a[...]
-    out[...] = dressed(left, right, mixed)
-
-
-def dress_b_kernel(steps, weights, left, right, one_b, two_b, pair_b, other, *rest):
-    absorb, emit = strengths(steps, weights)
-    odd, _, one, two = place()
-    mixed = kept(one, one_b[...]) + kept(two, two_b[...]) + jnp.where(odd, absorb[0], emit[0]) * pair_b[...]
-    out = rest[-1]
-    out[0] = other[...] + dressed(left, right, mixed)
-
-
-def vertex_left_kernel(vertex, left_a, left_b):
-    half = left_a.shape[1] // 3
+    mixed_a = from_one * kept(one, one_a[...]) + from_two * kept(two, two_a[...]) + across_a[...]
+    mixed_b = (
+        kept(one, one_b[...]) + kept(two, two_b[...]) + jnp.where(odd, absorb[0], emit[0]) * pair_b[...]
+    )
+    high, low = split(jnp.concatenate([mixed_a, mixed_b], axis=0))
+    high, low = split(dot(left[...], jnp.concatenate([high, low, high], axis=0)))
+    outer = jnp.concatenate([high, high, low], axis=1)
+    half = mixed_a.shape[0]
+    copies = []
+    for piece in (0, 1):
+        rows = pl.ds(piece * half, half)
+        held_out[rows] = dot(outer[piece * half : piece * half + half], right[...])
+        copies.append(pltpu.make_async_copy(held_out.at[rows], out.at[at, rows], sent.at[piece]))
+        copies[-1].start()
+    for copy in copies:
+        copy.wait()
+
+
+def vertex_left_kernel(vertex, left):
     high, low = split(vertex[...])
-    for side, left in enumerate((left_a, left_b)):
-        part = (slice(None), slice(side * half, side * half + half))
-        left[...] = jnp.concatenate([high[part], high[part], low[part]], axis=1)
+    left[...] = jnp.concatenate([high, high, low], axis=1)
 
 
 def vertex_right_kernel(vertex, right):
@@ -396,8 +393,9 @@
         one_b = exchange(one_b, in_one)
         across_a = exchange(across_a, in_pair)
         combined.append((across_a, one_b, two_b))
-    lefts = jax.ShapeDtypeStruct((size, 3 * half), BF16)
-    left_a, left_b = call(vertex_left_kernel, [lefts, lefts], [phonon_vertex[0]])
+    left = call(
+        vertex_left_kernel, jax.ShapeDtypeStruct((size, 3 * size), BF16), [phonon_vertex[0]]
+    )
     right = call(
         vertex_right_kernel, jax.ShapeDtypeStruct((3 * size, size), BF16), [phonon_vertex[0]]
     )
@@ -405,14 +403,7 @@
     for at, (part, more) in enumerate(zip(parts, combined)):
         _, _, one_a, two_a, pair_b = part
         across_a, one_b, two_b = more
-        other = call(
-            dress_a_kernel,
-            held(size, size),
-            [mode_steps, mode_weights, left_a, right, one_a, two_a, across_a],
-            scalars=2,
-            flops=cube // 8,
-        )
-        args = [mode_steps, mode_weights, left_b, right, one_b, two_b, pair_b, other]
+        args = [mode_steps, mode_weights, left, right, one_a, two_a, across_a, one_b, two_b, pair_b]
         vmem = pl.BlockSpec(memory_space=pltpu.VMEM)
         specs = [pl.BlockSpec(memory_space=pltpu.SMEM)] * 2 + [vmem] * (len(args) - 2)
         aliases = {}
@@ -420,13 +411,13 @@
             aliases = {len(args): 0}
             args, specs = [*args, out], [*specs, pl.BlockSpec(memory_space=pl.ANY)]
         out = call(
-            dress_b_kernel,
+            functools.partial(dress_kernel, at),
             held(2, size, size),
             args,
-            flops=cube // 8,
+            flops=cube // 4,
             in_specs=specs,
-            grid=(1,),
-            out_specs=pl.BlockSpec((1, size, size), functools.partial(lambda at, i: (at, 0, 0), at)),
+            out_specs=pl.BlockSpec(memory_space=pl.ANY),
+            scratch_shapes=[pltpu.VMEM((size, size), F32), pltpu.SemaphoreType.DMA((2,))],
             input_output_aliases=aliases,
         )
     return out.reshape(old_sigma.shape)

time: 53.6 us -> 50.2 us (0.937); the launches traced: 53.5 us -> 49.5 us
  Pallas kernels: 22.2 us -> 20 us
  waiting for transfers between devices: 12.7 us -> 11.2 us
    pallas_call x13 -> x11, Pallas kernels: 22.2 us -> 20 us  [call(): pl.pallas_call(kernel, out_shape=outs, compiler_params=pltpu.CompilerPara...]
    ppermute x12, waiting for transfers between devices: 12.2 us -> 10.7 us  [exchange(): return lax.ppermute(x, ('slab', 'energy'), pairs)]
  transfers between devices with their start and end apart: 14 -> 14, of which waited for: 7 -> 7; matrix products, arithmetic and copies ran while one was open for 0% -> 0% of each run, Pallas kernels for 22% -> 19%
where the time goes in v1:
time: 50.2 us; the launch traced here: 49.5 us
  Pallas kernels  20 us (40%)
  starting transfers between devices  18.1 us (36%)
  waiting for transfers between devices  11.2 us (22%)
    pallas_call x11, Pallas kernels, call(): pl.pallas_call(kernel, out_shape=outs, compiler_params=pltpu.CompilerPara...  20 us
    ppermute x12, starting transfers between devices, exchange(): return lax.ppermute(x, ('slab', 'energy'), pairs)  15 us
    ppermute x12, waiting for transfers between devices, exchange(): return lax.ppermute(x, ('slab', 'energy'), pairs)  10.7 us
    ppermute x2, starting transfers between devices, per_device(): far = lax.ppermute(near, 'slab', [(i, i ^ reach) for i in range(slabs)])  3.11 us
  transfers between devices with their start and end apart: 14, of which 7 were waited for; matrix products, arithmetic and copies ran while one was open for 0% of the time, Pallas kernels for 19%

profile of v1, /device:TPU:0, one launch (start us, length us, event | category | flops | bytes accessed | tf_op | source)
XLA Modules:
  0.0 49.5 jit_solution(14936541005667415065)
XLA Ops:
  0.0 6.1 %shard_map.93 = (f32[384,768]{1,0:T(8,128)S(1)}, f32[384,768]{1,0:T(8,128)S(1)}, f32[384,2]{1,0:T(8,128)S(1)}, f32[128,768]{1,0:T(8,128)S(1)}, f32[128,256]{1,0:T(8,128)S(1)}) custom-call(f32[1,384]{1,0:T(1,128)} %refs_0_.1, f32[384,384]{1,0:T(8,128)} %bitcast.9, f32[2,384,384]{2,1,0:T(8,128)} %bitcast.8, f32[1,128]{1,0:T(1,128)} %coupling.1, s32[1,128]{1,0:T(1,128)} %bound.1), custom_call_target="tpu_custom_call" | custom-call | flops 2717908992 | bytes 4658688 | tf_op jit(solution)/shard_map/pallas_call | solution.py:292
  6.1 3.0 %collective-permute-start = (f32[128,256]{1,0:T(8,128)S(1)}, f32[128,256]{1,0:T(8,128)S(1)}, u32[]{:S(2)}, u32[]{:S(2)}) collective-permute-start(f32[128,256]{1,0:T(8,128)S(1)} %get-tuple-element.29), channel_id=1, source_target_pairs={{0,16},{8,24},{16,0},{24,8},{1,17},{9,25},{17,1},{25,9},{2,18},{10... | collective-permute-start | bytes 393224 | tf_op jit(solution)/shard_map/ppermute | solution.py:368
  9.2 3.0 %shard_map.94 = (f32[384,768]{1,0:T(8,128)S(1)}, f32[384,768]{1,0:T(8,128)S(1)}) custom-call(f32[384,768]{1,0:T(8,128)S(1)} %get-tuple-element.25.first, f32[384,768]{1,0:T(8,128)S(1)} %get-tuple-element.26.second, f32[384,2]{1,0:T(8,128)S(1)} %get-tuple-element.27.start), custom_call_target="tpu_custom_call" | custom-call | flops 2717908992 | bytes 4721664 | tf_op jit(solution)/shard_map/pallas_call | solution.py:292
  12.2 0.5 %collective-permute-done = f32[128,256]{1,0:T(8,128)S(1)} collective-permute-done((f32[128,256]{1,0:T(8,128)S(1)}, f32[128,256]{1,0:T(8,128)S(1)}, u32[]{:S(2)}, u32[]{:S(2)}) %collective-permute-start) | collective-permute-done | bytes 131104 | tf_op jit(solution)/shard_map/ppermute | solution.py:368
  12.7 0.1 collective-permute-start.1
  12.8 0.0 copy-start.3
  12.8 0.0 copy-start.4
  12.8 0.0 copy-start.5
  12.8 1.6 %shard_map.95.inverse = f32[384,768]{1,0:T(8,128)S(1)} custom-call(f32[384,768]{1,0:T(8,128)S(1)} %get-tuple-element.28.partial, f32[384,768]{1,0:T(8,128)S(1)} %get-tuple-element.31.fourth), custom_call_target="tpu_custom_call" | custom-call | flops 1358954496 | bytes 3538944 | tf_op jit(solution)/shard_map/pallas_call | solution.py:292
  14.3 0.0 collective-permute-done.1.far
  14.4 0.0 copy-done.3
  14.4 0.0 copy-done.4
  14.4 0.0 copy-done.5
  14.4 1.8 %shard_map.96 = (f32[384,256]{1,0:T(8,128)S(1)}, f32[192,384]{1,0:T(8,128)S(1)}, f32[192,384]{1,0:T(8,128)S(1)}) custom-call(f32[128,128]{1,0:T(8,128)S(1)} %copy-done.3, f32[1,128]{1,0:T(1,128)S(1)} %copy-done.4, s32[1,128]{1,0:T(1,128)S(1)} %copy-done.5, f32[384,768]{1,0:T(8,128)S(1)} %shard_map.95.inverse, f32[128,768]{1,0:T(8,128)S(1)} %get-tuple-element.32.rows, ...), custom_call_target="tpu_custom_call" | custom-call | flops 1358954496 | bytes 2884608 | tf_op jit(solution)/shard_map/pallas_call | solution.py:292
  16.2 0.0 copy-start.1
  16.2 0.0 copy-start.2
  16.3 1.8 %collective-permute-start.10 = (f32[192,384]{1,0:T(8,128)S(1)}, f32[192,384]{1,0:T(8,128)S(1)}, u32[]{:S(2)}, u32[]{:S(2)}) collective-permute-start(f32[192,384]{1,0:T(8,128)S(1)} %get-tuple-element.41.green_b), channel_id=1, source_target_pairs={{0,1},{1,0},{2,3},{3,2},{4,5},{5,4},{6,7},{7,6},{8,9},{9,8},{10,11... | collective-permute-start | bytes 884744 | tf_op jit(solution)/shard_map/ppermute | solution.py:316
  18.1 1.6 %collective-permute-start.8 = (f32[192,384]{1,0:T(8,128)S(1)}, f32[192,384]{1,0:T(8,128)S(1)}, u32[]{:S(2)}, u32[]{:S(2)}) collective-permute-start(f32[192,384]{1,0:T(8,128)S(1)} %get-tuple-element.40.green_a), channel_id=1, source_target_pairs={{0,2},{1,3},{2,0},{3,1},{4,6},{5,7},{6,4},{7,5},{8,10},{9,11},{10,... | collective-permute-start | bytes 884744 | tf_op jit(solution)/shard_map/ppermute | solution.py:316
  19.7 0.0 collective-permute-start.9
  19.7 0.5 shard_map.97
  20.2 3.2 %collective-permute-start.2 = (f32[192,384]{1,0:T(8,128)S(1)}, f32[192,384]{1,0:T(8,128)S(1)}, u32[]{:S(2)}, u32[]{:S(2)}) collective-permute-start(f32[192,384]{1,0:T(8,128)S(1)} %get-tuple-element.35.green_a), channel_id=1, source_target_pairs={{0,2},{1,3},{2,0},{3,1},{4,6},{5,7},{6,4},{7,5},{8,10},{9,11},{10,... | collective-permute-start | bytes 884744 | tf_op jit(solution)/shard_map/ppermute | solution.py:316
  23.4 0.0 collective-permute-start.3
  23.4 2.4 %collective-permute-done.10.pair_b = f32[192,384]{1,0:T(8,128)S(1)} collective-permute-done((f32[192,384]{1,0:T(8,128)S(1)}, f32[192,384]{1,0:T(8,128)S(1)}, u32[]{:S(2)}, u32[]{:S(2)}) %collective-permute-start.10) | collective-permute-done | bytes 294944 | tf_op jit(solution)/shard_map/ppermute | solution.py:316
  25.7 1.7 %collective-permute-start.4 = (f32[192,384]{1,0:T(8,128)S(1)}, f32[192,384]{1,0:T(8,128)S(1)}, u32[]{:S(2)}, u32[]{:S(2)}) collective-permute-start(f32[192,384]{1,0:T(8,128)S(1)} %get-tuple-element.36.green_b), channel_id=1, source_target_pairs={{0,1},{1,0},{2,3},{3,2},{4,5},{5,4},{6,7},{7,6},{8,9},{9,8},{10,11... | collective-permute-start | bytes 884744 | tf_op jit(solution)/shard_map/ppermute | solution.py:316
  27.5 0.5 %collective-permute-done.8.one_a = f32[192,384]{1,0:T(8,128)S(1)} collective-permute-done((f32[192,384]{1,0:T(8,128)S(1)}, f32[192,384]{1,0:T(8,128)S(1)}, u32[]{:S(2)}, u32[]{:S(2)}) %collective-permute-start.8) | collective-permute-done | bytes 294944 | tf_op jit(solution)/shard_map/ppermute | solution.py:316
  28.0 0.0 collective-permute-done.9.two_a
  28.0 0.0 copy-done.2
  28.0 0.7 %shard_map.99 = (f32[192,384]{1,0:T(8,128)S(1)}, f32[192,384]{1,0:T(8,128)S(1)}, f32[192,384]{1,0:T(8,128)S(1)}) custom-call(s32[2]{0:T(128)S(1)} %copy-done.2, f32[2,2]{1,0:T(2,128)S(1)} %copy-done.1, f32[192,384]{1,0:T(8,128)S(1)} %get-tuple-element.40.green_a, f32[192,384]{1,0:T(8,128)S(1)} %get-tuple-element.41.green_b, ...), custom_call_target="tpu_custom_call" | custom-call | bytes 2359320 | tf_op jit(solution)/shard_map/pallas_call | solution.py:292
  28.7 0.3 collective-permute-start.11
  29.0 2.9 %collective-permute-start.12 = (f32[192,384]{1,0:T(8,128)S(1)}, f32[192,384]{1,0:T(8,128)S(1)}, u32[]{:S(2)}, u32[]{:S(2)}) collective-permute-start(f32[192,384]{1,0:T(8,128)S(1)} %get-tuple-element.43), channel_id=1, source_target_pairs={{0,2},{1,3},{2,0},{3,1},{4,6},{5,7},{6,4},{7,5},{8,10},{9,11},{10,... | collective-permute-start | bytes 884744 | tf_op jit(solution)/shard_map/ppermute | solution.py:316
  32.0 2.3 %collective-permute-done.2.one_a = f32[192,384]{1,0:T(8,128)S(1)} collective-permute-done((f32[192,384]{1,0:T(8,128)S(1)}, f32[192,384]{1,0:T(8,128)S(1)}, u32[]{:S(2)}, u32[]{:S(2)}) %collective-permute-start.2) | collective-permute-done | bytes 294944 | tf_op jit(solution)/shard_map/ppermute | solution.py:316
  34.3 0.0 collective-permute-start.13
  34.3 0.0 collective-permute-done.3.two_a
  34.3 1.3 %collective-permute-done.4.pair_b = f32[192,384]{1,0:T(8,128)S(1)} collective-permute-done((f32[192,384]{1,0:T(8,128)S(1)}, f32[192,384]{1,0:T(8,128)S(1)}, u32[]{:S(2)}, u32[]{:S(2)}) %collective-permute-start.4) | collective-permute-done | bytes 294944 | tf_op jit(solution)/shard_map/ppermute | solution.py:316
  35.6 0.7 %shard_map.98 = (f32[192,384]{1,0:T(8,128)S(1)}, f32[192,384]{1,0:T(8,128)S(1)}, f32[192,384]{1,0:T(8,128)S(1)}) custom-call(s32[2]{0:T(128)S(1)} %copy-done.2, f32[2,2]{1,0:T(2,128)S(1)} %copy-done.1, f32[192,384]{1,0:T(8,128)S(1)} %get-tuple-element.35.green_a, f32[192,384]{1,0:T(8,128)S(1)} %get-tuple-element.36.green_b, ...), custom_call_target="tpu_custom_call" | custom-call | bytes 2359320 | tf_op jit(solution)/shard_map/pallas_call | solution.py:292
  36.3 1.8 %collective-permute-start.5 = (f32[192,384]{1,0:T(8,128)S(1)}, f32[192,384]{1,0:T(8,128)S(1)}, u32[]{:S(2)}, u32[]{:S(2)}) collective-permute-start(f32[192,384]{1,0:T(8,128)S(1)} %get-tuple-element.37), channel_id=1, source_target_pairs={{0,1},{1,0},{2,3},{3,2},{4,5},{5,4},{6,7},{7,6},{8,9},{9,8},{10,11... | collective-permute-start | bytes 884744 | tf_op jit(solution)/shard_map/ppermute | solution.py:316
  38.1 1.6 %collective-permute-start.6 = (f32[192,384]{1,0:T(8,128)S(1)}, f32[192,384]{1,0:T(8,128)S(1)}, u32[]{:S(2)}, u32[]{:S(2)}) collective-permute-start(f32[192,384]{1,0:T(8,128)S(1)} %get-tuple-element.38), channel_id=1, source_target_pairs={{0,2},{1,3},{2,0},{3,1},{4,6},{5,7},{6,4},{7,5},{8,10},{9,11},{10,... | collective-permute-start | bytes 884744 | tf_op jit(solution)/shard_map/ppermute | solution.py:316
  39.7 2.2 %collective-permute-done.11.across_a = f32[192,384]{1,0:T(8,128)S(1)} collective-permute-done((f32[192,384]{1,0:T(8,128)S(1)}, f32[192,384]{1,0:T(8,128)S(1)}, u32[]{:S(2)}, u32[]{:S(2)}) %collective-permute-start.11) | collective-permute-done | bytes 294944 | tf_op jit(solution)/shard_map/ppermute | solution.py:316
  41.9 0.0 collective-permute-start.7
  41.9 0.1 shard_map.91.left
  42.0 0.2 shard_map.92.right
  42.3 0.0 collective-permute-done.12.one_b
  42.3 0.0 collective-permute-done.13.two_b
  42.3 2.6 %shard_map.100.rest_0_ = f32[2,384,384]{2,1,0:T(8,128)} custom-call(s32[2]{0:T(128)S(1)} %copy-done.2, f32[2,2]{1,0:T(2,128)S(1)} %copy-done.1, bf16[384,1152]{1,0:T(8,128)(2,1)S(1)} %shard_map.91.left, bf16[1152,384]{1,0:T(8,128)(2,1)S(1)} %shard_map.92.right, f32[192,384]{1,0:T(8,128)S(1)} %collective-permute-done.8.one_a, ...), custom_call_target="tpu_custom_call" | custom-call | flops 339738624 | bytes 6488088 | tf_op jit(solution)/shard_map/pallas_call | solution.py:292
  44.9 2.0 %collective-permute-done.5.across_a = f32[192,384]{1,0:T(8,128)S(1)} collective-permute-done((f32[192,384]{1,0:T(8,128)S(1)}, f32[192,384]{1,0:T(8,128)S(1)}, u32[]{:S(2)}, u32[]{:S(2)}) %collective-permute-start.5) | collective-permute-done | bytes 294944 | tf_op jit(solution)/shard_map/ppermute | solution.py:316
  46.9 0.0 collective-permute-done.6.one_b
  46.9 0.0 collective-permute-done.7.two_b
  46.9 2.6 %shard_map.101 = f32[2,384,384]{2,1,0:T(8,128)} custom-call(s32[2]{0:T(128)S(1)} %copy-done.2, f32[2,2]{1,0:T(2,128)S(1)} %copy-done.1, bf16[384,1152]{1,0:T(8,128)(2,1)S(1)} %shard_map.91.left, bf16[1152,384]{1,0:T(8,128)(2,1)S(1)} %shard_map.92.right, f32[192,384]{1,0:T(8,128)S(1)} %collective-permute-done.2.one_a, ...), custom_call_target="tpu_custom_call", output_to_operand_aliasing={{}: (10, {})} | custom-call | flops 339738624 | bytes 7667736 | tf_op jit(solution)/shard_map/pallas_call | solution.py:292
  (4 shorter events, 0.0 us)
Async XLA Ops:
  6.1 6.5 %collective-permute-start = (f32[128,256]{1,0:T(8,128)S(1)}, f32[128,256]{1,0:T(8,128)S(1)}, u32[]{:S(2)}, u32[]{:S(2)}) collective-permute-start(f32[128,256]{1,0:T(8,128)S(1)} %get-tuple-element.29), channel_id=1, source_target_pairs={{0,16},{8,24},{16,0},{24,8},{1,17},{9,25},{17,1},{25,9},{2,18},{10... | collective-permute-start | bytes 393224 | tf_op jit(solution)/shard_map/ppermute | solution.py:368
  12.7 1.7 %collective-permute-start.1 = (f32[128,256]{1,0:T(8,128)S(1)}, f32[128,256]{1,0:T(8,128)S(1)}, u32[]{:S(2)}, u32[]{:S(2)}) collective-permute-start(f32[128,256]{1,0:T(8,128)S(1)} %add.3.near), channel_id=1, source_target_pairs={{0,8},{8,0},{16,24},{24,16},{1,9},{9,1},{17,25},{25,17},{2,10},{10... | collective-permute-start | bytes 393224 | tf_op jit(solution)/shard_map/ppermute | solution.py:368
  12.8 1.6 %copy-start.3 = (f32[128,128]{1,0:T(8,128)S(1)}, f32[128,128]{1,0:T(8,128)}, u32[]{:S(2)}) copy-start(f32[128,128]{1,0:T(8,128)} %hamiltonian.1) | copy-start | bytes 196612
  12.8 1.6 %copy-start.4 = (f32[1,128]{1,0:T(1,128)S(1)}, f32[1,128]{1,0:T(1,128)}, u32[]{:S(2)}) copy-start(f32[1,128]{1,0:T(1,128)} %coupling.1) | copy-start | bytes 1540
  12.8 1.6 %copy-start.5 = (s32[1,128]{1,0:T(1,128)S(1)}, s32[1,128]{1,0:T(1,128)}, u32[]{:S(2)}) copy-start(s32[1,128]{1,0:T(1,128)} %bound.1) | copy-start | bytes 1540
  16.2 11.7 %copy-start.1 = (f32[2,2]{1,0:T(2,128)S(1)}, f32[2,2]{1,0:T(2,128)}, u32[]{:S(2)}) copy-start(f32[2,2]{1,0:T(2,128)} %weights.7) | copy-start | bytes 52
  16.2 11.7 %copy-start.2 = (s32[2]{0:T(128)S(1)}, s32[2]{0:T(128)}, u32[]{:S(2)}) copy-start(s32[2]{0:T(128)} %steps.7) | copy-start | bytes 28
  16.3 9.5 %collective-permute-start.10 = (f32[192,384]{1,0:T(8,128)S(1)}, f32[192,384]{1,0:T(8,128)S(1)}, u32[]{:S(2)}, u32[]{:S(2)}) collective-permute-start(f32[192,384]{1,0:T(8,128)S(1)} %get-tuple-element.41.green_b), channel_id=1, source_target_pairs={{0,1},{1,0},{2,3},{3,2},{4,5},{5,4},{6,7},{7,6},{8,9},{9,8},{10,11... | collective-permute-start | bytes 884744 | tf_op jit(solution)/shard_map/ppermute | solution.py:316
  18.1 9.9 %collective-permute-start.8 = (f32[192,384]{1,0:T(8,128)S(1)}, f32[192,384]{1,0:T(8,128)S(1)}, u32[]{:S(2)}, u32[]{:S(2)}) collective-permute-start(f32[192,384]{1,0:T(8,128)S(1)} %get-tuple-element.40.green_a), channel_id=1, source_target_pairs={{0,2},{1,3},{2,0},{3,1},{4,6},{5,7},{6,4},{7,5},{8,10},{9,11},{10,... | collective-permute-start | bytes 884744 | tf_op jit(solution)/shard_map/ppermute | solution.py:316
  19.7 8.3 %collective-permute-start.9 = (f32[192,384]{1,0:T(8,128)S(1)}, f32[192,384]{1,0:T(8,128)S(1)}, u32[]{:S(2)}, u32[]{:S(2)}) collective-permute-start(f32[192,384]{1,0:T(8,128)S(1)} %get-tuple-element.40.green_a), channel_id=1, source_target_pairs={{0,8},{1,9},{2,4},{3,5},{4,2},{5,3},{6,14},{7,15},{8,0},{9,1},{10,... | collective-permute-start | bytes 884744 | tf_op jit(solution)/shard_map/ppermute | solution.py:316
  20.2 14.1 %collective-permute-start.2 = (f32[192,384]{1,0:T(8,128)S(1)}, f32[192,384]{1,0:T(8,128)S(1)}, u32[]{:S(2)}, u32[]{:S(2)}) collective-permute-start(f32[192,384]{1,0:T(8,128)S(1)} %get-tuple-element.35.green_a), channel_id=1, source_target_pairs={{0,2},{1,3},{2,0},{3,1},{4,6},{5,7},{6,4},{7,5},{8,10},{9,11},{10,... | collective-permute-start | bytes 884744 | tf_op jit(solution)/shard_map/ppermute | solution.py:316
  23.4 10.9 %collective-permute-start.3 = (f32[192,384]{1,0:T(8,128)S(1)}, f32[192,384]{1,0:T(8,128)S(1)}, u32[]{:S(2)}, u32[]{:S(2)}) collective-permute-start(f32[192,384]{1,0:T(8,128)S(1)} %get-tuple-element.35.green_a), channel_id=1, source_target_pairs={{0,8},{1,9},{2,4},{3,5},{4,2},{5,3},{6,14},{7,15},{8,0},{9,1},{10,... | collective-permute-start | bytes 884744 | tf_op jit(solution)/shard_map/ppermute | solution.py:316
  25.7 16.2 %copy-start = (f32[1,384,384]{2,1,0:T(8,128)S(1)}, f32[1,384,384]{2,1,0:T(8,128)}, u32[]{:S(2)}) copy-start(f32[1,384,384]{2,1,0:T(8,128)} %param.15) | copy-start | bytes 1769476
  25.7 9.9 %collective-permute-start.4 = (f32[192,384]{1,0:T(8,128)S(1)}, f32[192,384]{1,0:T(8,128)S(1)}, u32[]{:S(2)}, u32[]{:S(2)}) collective-permute-start(f32[192,384]{1,0:T(8,128)S(1)} %get-tuple-element.36.green_b), channel_id=1, source_target_pairs={{0,1},{1,0},{2,3},{3,2},{4,5},{5,4},{6,7},{7,6},{8,9},{9,8},{10,11... | collective-permute-start | bytes 884744 | tf_op jit(solution)/shard_map/ppermute | solution.py:316
  28.7 13.2 %collective-permute-start.11 = (f32[192,384]{1,0:T(8,128)S(1)}, f32[192,384]{1,0:T(8,128)S(1)}, u32[]{:S(2)}, u32[]{:S(2)}) collective-permute-start(f32[192,384]{1,0:T(8,128)S(1)} %get-tuple-element.42), channel_id=1, source_target_pairs={{0,1},{1,0},{2,3},{3,2},{4,5},{5,4},{6,7},{7,6},{8,9},{9,8},{10,11... | collective-permute-start | bytes 884744 | tf_op jit(solution)/shard_map/ppermute | solution.py:316
  29.0 13.2 %collective-permute-start.12 = (f32[192,384]{1,0:T(8,128)S(1)}, f32[192,384]{1,0:T(8,128)S(1)}, u32[]{:S(2)}, u32[]{:S(2)}) collective-permute-start(f32[192,384]{1,0:T(8,128)S(1)} %get-tuple-element.43), channel_id=1, source_target_pairs={{0,2},{1,3},{2,0},{3,1},{4,6},{5,7},{6,4},{7,5},{8,10},{9,11},{10,... | collective-permute-start | bytes 884744 | tf_op jit(solution)/shard_map/ppermute | solution.py:316
  34.3 8.0 %collective-permute-start.13 = (f32[192,384]{1,0:T(8,128)S(1)}, f32[192,384]{1,0:T(8,128)S(1)}, u32[]{:S(2)}, u32[]{:S(2)}) collective-permute-start(f32[192,384]{1,0:T(8,128)S(1)} %get-tuple-element.44), channel_id=1, source_target_pairs={{0,8},{1,9},{2,4},{3,5},{4,2},{5,3},{6,14},{7,15},{8,0},{9,1},{10,... | collective-permute-start | bytes 884744 | tf_op jit(solution)/shard_map/ppermute | solution.py:316
  36.3 10.6 %collective-permute-start.5 = (f32[192,384]{1,0:T(8,128)S(1)}, f32[192,384]{1,0:T(8,128)S(1)}, u32[]{:S(2)}, u32[]{:S(2)}) collective-permute-start(f32[192,384]{1,0:T(8,128)S(1)} %get-tuple-element.37), channel_id=1, source_target_pairs={{0,1},{1,0},{2,3},{3,2},{4,5},{5,4},{6,7},{7,6},{8,9},{9,8},{10,11... | collective-permute-start | bytes 884744 | tf_op jit(solution)/shard_map/ppermute | solution.py:316
  38.1 8.8 %collective-permute-start.6 = (f32[192,384]{1,0:T(8,128)S(1)}, f32[192,384]{1,0:T(8,128)S(1)}, u32[]{:S(2)}, u32[]{:S(2)}) collective-permute-start(f32[192,384]{1,0:T(8,128)S(1)} %get-tuple-element.38), channel_id=1, source_target_pairs={{0,2},{1,3},{2,0},{3,1},{4,6},{5,7},{6,4},{7,5},{8,10},{9,11},{10,... | collective-permute-start | bytes 884744 | tf_op jit(solution)/shard_map/ppermute | solution.py:316
  41.9 5.0 %collective-permute-start.7 = (f32[192,384]{1,0:T(8,128)S(1)}, f32[192,384]{1,0:T(8,128)S(1)}, u32[]{:S(2)}, u32[]{:S(2)}) collective-permute-start(f32[192,384]{1,0:T(8,128)S(1)} %get-tuple-element.39), channel_id=1, source_target_pairs={{0,8},{1,9},{2,4},{3,5},{4,2},{5,3},{6,14},{7,15},{8,0},{9,1},{10,... | collective-permute-start | bytes 884744 | tf_op jit(solution)/shard_map/ppermute | solution.py:316

commit v2 on v1

--- a/solution.py
+++ b/solution.py
@@ -205,9 +205,10 @@
     absorb, emit = [], []
     for distance in (1, 2):
         for row, out in ((0, absorb), (1, emit)):
-            total = jnp.float32(0.0)
-            for mode in range(steps.shape[0]):
-                total = total + jnp.where(steps[mode] == distance, weights[row, mode], 0.0)
+            total = jnp.zeros((1, 1), F32)
+            for mode in range(steps.shape[1]):
+                at = slice(mode, mode + 1)
+                total = total + jnp.where(steps[:, at] == distance, weights[row : row + 1, at], 0.0)
             out.append(total)
     return absorb, emit
 
@@ -229,7 +230,7 @@
 def combine_kernel(steps, weights, green_a, green_b, one_a, two_a, pair_b, across_a, one_b, two_b):
     absorb, emit = strengths(steps, weights)
     odd, odd_pair, one, two = place()
-    zero = jnp.float32(0.0)
+    zero = jnp.zeros((1, 1), F32)
     from_one = jnp.where(odd, jnp.where(odd_pair, absorb[0], zero), jnp.where(odd_pair, zero, emit[0]))
     from_two = jnp.where(odd, jnp.where(odd_pair, zero, absorb[0]), jnp.where(odd_pair, emit[0], zero))
     across_a[...] = (
@@ -280,12 +281,11 @@
         right[at * size : (at + 1) * size, :] = part
 
 
-def call(kernel, outs, args, scalars=0, flops=0, **kept):
+def call(kernel, outs, args, flops=0, **kept):
     vmem = pl.BlockSpec(memory_space=pltpu.VMEM)
-    smem = pl.BlockSpec(memory_space=pltpu.SMEM)
     touched = sum(4 * a.size for a in [*args, *jax.tree.leaves(outs)])
     settings = dict(
-        in_specs=[smem] * scalars + [vmem] * (len(args) - scalars),
+        in_specs=[vmem] * len(args),
         out_specs=jax.tree.map(lambda _: vmem, outs),
     )
     settings.update(kept)
@@ -346,6 +346,7 @@
     cube = 3 * 8 * size**3
     full = held(size, 2 * size)
     sigma = old_sigma.reshape(2, size, size)
+    mode_steps = mode_steps[None]
     given = [
         pltpu.with_memory_space_constraint(x, pltpu.HBM)
         for x in (onsite, hopping[0], sigma, coupling, bound_rows)
@@ -387,7 +388,7 @@
     combined = []
     for part in parts:
         across_a, one_b, two_b = call(
-            combine_kernel, [held(half, size)] * 3, [mode_steps, mode_weights, *part], scalars=2
+            combine_kernel, [held(half, size)] * 3, [mode_steps, mode_weights, *part]
         )
         two_b = exchange(two_b, in_two)
         one_b = exchange(one_b, in_one)
@@ -405,7 +406,7 @@
         across_a, one_b, two_b = more
         args = [mode_steps, mode_weights, left, right, one_a, two_a, across_a, one_b, two_b, pair_b]
         vmem = pl.BlockSpec(memory_space=pltpu.VMEM)
-        specs = [pl.BlockSpec(memory_space=pltpu.SMEM)] * 2 + [vmem] * (len(args) - 2)
+        specs = [vmem] * len(args)
         aliases = {}
         if out is not None:
             aliases = {len(args): 0}

time: 50.2 us -> 49.7 us (0.990)
  Pallas kernels: 20 us -> 18.4 us
  waiting for transfers between devices: 11.2 us -> 12.3 us
    pallas_call x11, Pallas kernels: 20 us -> 18.4 us  [call(): pl.pallas_call(kernel, out_shape=outs, compiler_params=pltpu.CompilerPara...]
    ppermute x12, waiting for transfers between devices: 10.7 us -> 11.8 us  [exchange(): return lax.ppermute(x, ('slab', 'energy'), pairs)]
  transfers between devices with their start and end apart: 14 -> 14, of which waited for: 7 -> 7; matrix products, arithmetic and copies ran while one was open for 0% -> 0% of each run, Pallas kernels for 19% -> 17%
where the time goes in v2:
time: 49.7 us; the launch traced here: 49.1 us
  Pallas kernels  18.4 us (37%)
  starting transfers between devices  18.1 us (36%)
  waiting for transfers between devices  12.3 us (25%)
    pallas_call x11, Pallas kernels, call(): pl.pallas_call(kernel, out_shape=outs, compiler_params=pltpu.CompilerPara...  18.4 us
    ppermute x12, starting transfers between devices, exchange(): return lax.ppermute(x, ('slab', 'energy'), pairs)  15 us
    ppermute x12, waiting for transfers between devices, exchange(): return lax.ppermute(x, ('slab', 'energy'), pairs)  11.8 us
    ppermute x2, starting transfers between devices, per_device(): far = lax.ppermute(near, 'slab', [(i, i ^ reach) for i in range(slabs)])  3.11 us
  transfers between devices with their start and end apart: 14, of which 7 were waited for; matrix products, arithmetic and copies ran while one was open for 0% of the time, Pallas kernels for 17%

profile of v2, /device:TPU:0, one launch (start us, length us, event | category | flops | bytes accessed | tf_op | source)
XLA Modules:
  0.0 49.1 jit_solution(12336619230377844707)
XLA Ops:
  0.0 6.1 %shard_map.93 = (f32[384,768]{1,0:T(8,128)S(1)}, f32[384,768]{1,0:T(8,128)S(1)}, f32[384,2]{1,0:T(8,128)S(1)}, f32[128,768]{1,0:T(8,128)S(1)}, f32[128,256]{1,0:T(8,128)S(1)}) custom-call(f32[1,384]{1,0:T(1,128)} %refs_0_.1, f32[384,384]{1,0:T(8,128)} %bitcast.14, f32[2,384,384]{2,1,0:T(8,128)} %bitcast.13, f32[1,128]{1,0:T(1,128)} %coupling.1, s32[1,128]{1,0:T(1,128)} %bound.1), custom_call_target="tpu_custom_call" | custom-call | flops 2717908992 | bytes 4658688 | tf_op jit(solution)/shard_map/pallas_call | solution.py:292
  6.1 3.0 %collective-permute-start = (f32[128,256]{1,0:T(8,128)S(1)}, f32[128,256]{1,0:T(8,128)S(1)}, u32[]{:S(2)}, u32[]{:S(2)}) collective-permute-start(f32[128,256]{1,0:T(8,128)S(1)} %get-tuple-element.29), channel_id=1, source_target_pairs={{0,16},{8,24},{16,0},{24,8},{1,17},{9,25},{17,1},{25,9},{2,18},{10... | collective-permute-start | bytes 393224 | tf_op jit(solution)/shard_map/ppermute | solution.py:369
  9.2 3.0 %shard_map.94 = (f32[384,768]{1,0:T(8,128)S(1)}, f32[384,768]{1,0:T(8,128)S(1)}) custom-call(f32[384,768]{1,0:T(8,128)S(1)} %get-tuple-element.25.first, f32[384,768]{1,0:T(8,128)S(1)} %get-tuple-element.26.second, f32[384,2]{1,0:T(8,128)S(1)} %get-tuple-element.27.start), custom_call_target="tpu_custom_call" | custom-call | flops 2717908992 | bytes 4721664 | tf_op jit(solution)/shard_map/pallas_call | solution.py:292
  12.2 0.5 %collective-permute-done = f32[128,256]{1,0:T(8,128)S(1)} collective-permute-done((f32[128,256]{1,0:T(8,128)S(1)}, f32[128,256]{1,0:T(8,128)S(1)}, u32[]{:S(2)}, u32[]{:S(2)}) %collective-permute-start) | collective-permute-done | bytes 131104 | tf_op jit(solution)/shard_map/ppermute | solution.py:369
  12.7 0.1 collective-permute-start.1
  12.8 0.0 copy-start.3
  12.8 0.0 copy-start.4
  12.8 0.0 copy-start.5
  12.8 1.6 %shard_map.95.inverse = f32[384,768]{1,0:T(8,128)S(1)} custom-call(f32[384,768]{1,0:T(8,128)S(1)} %get-tuple-element.28.partial, f32[384,768]{1,0:T(8,128)S(1)} %get-tuple-element.31.fourth), custom_call_target="tpu_custom_call" | custom-call | flops 1358954496 | bytes 3538944 | tf_op jit(solution)/shard_map/pallas_call | solution.py:292
  14.3 0.0 collective-permute-done.1.far
  14.4 0.0 copy-done.3
  14.4 0.0 copy-done.4
  14.4 0.0 copy-done.5
  14.4 1.8 %shard_map.96 = (f32[384,256]{1,0:T(8,128)S(1)}, f32[192,384]{1,0:T(8,128)S(1)}, f32[192,384]{1,0:T(8,128)S(1)}) custom-call(f32[128,128]{1,0:T(8,128)S(1)} %copy-done.3, f32[1,128]{1,0:T(1,128)S(1)} %copy-done.4, s32[1,128]{1,0:T(1,128)S(1)} %copy-done.5, f32[384,768]{1,0:T(8,128)S(1)} %shard_map.95.inverse, f32[128,768]{1,0:T(8,128)S(1)} %get-tuple-element.32.rows, ...), custom_call_target="tpu_custom_call" | custom-call | flops 1358954496 | bytes 2884608 | tf_op jit(solution)/shard_map/pallas_call | solution.py:292
  16.2 0.0 copy-start.1
  16.2 0.0 copy-start.2
  16.3 1.8 %collective-permute-start.10 = (f32[192,384]{1,0:T(8,128)S(1)}, f32[192,384]{1,0:T(8,128)S(1)}, u32[]{:S(2)}, u32[]{:S(2)}) collective-permute-start(f32[192,384]{1,0:T(8,128)S(1)} %get-tuple-element.41.green_b), channel_id=1, source_target_pairs={{0,1},{1,0},{2,3},{3,2},{4,5},{5,4},{6,7},{7,6},{8,9},{9,8},{10,11... | collective-permute-start | bytes 884744 | tf_op jit(solution)/shard_map/ppermute | solution.py:316
  18.1 1.6 %collective-permute-start.8 = (f32[192,384]{1,0:T(8,128)S(1)}, f32[192,384]{1,0:T(8,128)S(1)}, u32[]{:S(2)}, u32[]{:S(2)}) collective-permute-start(f32[192,384]{1,0:T(8,128)S(1)} %get-tuple-element.40.green_a), channel_id=1, source_target_pairs={{0,2},{1,3},{2,0},{3,1},{4,6},{5,7},{6,4},{7,5},{8,10},{9,11},{10,... | collective-permute-start | bytes 884744 | tf_op jit(solution)/shard_map/ppermute | solution.py:316
  19.7 0.0 collective-permute-start.9
  19.7 0.5 shard_map.97
  20.2 3.2 %collective-permute-start.2 = (f32[192,384]{1,0:T(8,128)S(1)}, f32[192,384]{1,0:T(8,128)S(1)}, u32[]{:S(2)}, u32[]{:S(2)}) collective-permute-start(f32[192,384]{1,0:T(8,128)S(1)} %get-tuple-element.35.green_a), channel_id=1, source_target_pairs={{0,2},{1,3},{2,0},{3,1},{4,6},{5,7},{6,4},{7,5},{8,10},{9,11},{10,... | collective-permute-start | bytes 884744 | tf_op jit(solution)/shard_map/ppermute | solution.py:316
  23.4 0.0 collective-permute-start.3
  23.4 2.4 %collective-permute-done.10.pair_b = f32[192,384]{1,0:T(8,128)S(1)} collective-permute-done((f32[192,384]{1,0:T(8,128)S(1)}, f32[192,384]{1,0:T(8,128)S(1)}, u32[]{:S(2)}, u32[]{:S(2)}) %collective-permute-start.10) | collective-permute-done | bytes 294944 | tf_op jit(solution)/shard_map/ppermute | solution.py:316
  25.7 1.7 %collective-permute-start.4 = (f32[192,384]{1,0:T(8,128)S(1)}, f32[192,384]{1,0:T(8,128)S(1)}, u32[]{:S(2)}, u32[]{:S(2)}) collective-permute-start(f32[192,384]{1,0:T(8,128)S(1)} %get-tuple-element.36.green_b), channel_id=1, source_target_pairs={{0,1},{1,0},{2,3},{3,2},{4,5},{5,4},{6,7},{7,6},{8,9},{9,8},{10,11... | collective-permute-start | bytes 884744 | tf_op jit(solution)/shard_map/ppermute | solution.py:316
  27.5 0.5 %collective-permute-done.8.one_a = f32[192,384]{1,0:T(8,128)S(1)} collective-permute-done((f32[192,384]{1,0:T(8,128)S(1)}, f32[192,384]{1,0:T(8,128)S(1)}, u32[]{:S(2)}, u32[]{:S(2)}) %collective-permute-start.8) | collective-permute-done | bytes 294944 | tf_op jit(solution)/shard_map/ppermute | solution.py:316
  28.0 0.0 collective-permute-done.9.two_a
  28.0 0.0 copy-start
  28.0 0.4 shard_map.99
  28.4 0.3 collective-permute-start.11
  28.7 2.9 %collective-permute-start.12 = (f32[192,384]{1,0:T(8,128)S(1)}, f32[192,384]{1,0:T(8,128)S(1)}, u32[]{:S(2)}, u32[]{:S(2)}) collective-permute-start(f32[192,384]{1,0:T(8,128)S(1)} %get-tuple-element.43), channel_id=1, source_target_pairs={{0,2},{1,3},{2,0},{3,1},{4,6},{5,7},{6,4},{7,5},{8,10},{9,11},{10,... | collective-permute-start | bytes 884744 | tf_op jit(solution)/shard_map/ppermute | solution.py:316
  31.6 2.7 %collective-permute-done.2.one_a = f32[192,384]{1,0:T(8,128)S(1)} collective-permute-done((f32[192,384]{1,0:T(8,128)S(1)}, f32[192,384]{1,0:T(8,128)S(1)}, u32[]{:S(2)}, u32[]{:S(2)}) %collective-permute-start.2) | collective-permute-done | bytes 294944 | tf_op jit(solution)/shard_map/ppermute | solution.py:316
  34.3 0.0 collective-permute-start.13
  34.3 0.0 collective-permute-done.3.two_a
  34.3 1.3 %collective-permute-done.4.pair_b = f32[192,384]{1,0:T(8,128)S(1)} collective-permute-done((f32[192,384]{1,0:T(8,128)S(1)}, f32[192,384]{1,0:T(8,128)S(1)}, u32[]{:S(2)}, u32[]{:S(2)}) %collective-permute-start.4) | collective-permute-done | bytes 294944 | tf_op jit(solution)/shard_map/ppermute | solution.py:316
  35.6 0.4 shard_map.98
  36.0 1.8 %collective-permute-start.5 = (f32[192,384]{1,0:T(8,128)S(1)}, f32[192,384]{1,0:T(8,128)S(1)}, u32[]{:S(2)}, u32[]{:S(2)}) collective-permute-start(f32[192,384]{1,0:T(8,128)S(1)} %get-tuple-element.37), channel_id=1, source_target_pairs={{0,1},{1,0},{2,3},{3,2},{4,5},{5,4},{6,7},{7,6},{8,9},{9,8},{10,11... | collective-permute-start | bytes 884744 | tf_op jit(solution)/shard_map/ppermute | solution.py:316
  37.8 1.6 %collective-permute-start.6 = (f32[192,384]{1,0:T(8,128)S(1)}, f32[192,384]{1,0:T(8,128)S(1)}, u32[]{:S(2)}, u32[]{:S(2)}) collective-permute-start(f32[192,384]{1,0:T(8,128)S(1)} %get-tuple-element.38), channel_id=1, source_target_pairs={{0,2},{1,3},{2,0},{3,1},{4,6},{5,7},{6,4},{7,5},{8,10},{9,11},{10,... | collective-permute-start | bytes 884744 | tf_op jit(solution)/shard_map/ppermute | solution.py:316
  39.3 2.6 %collective-permute-done.11.across_a = f32[192,384]{1,0:T(8,128)S(1)} collective-permute-done((f32[192,384]{1,0:T(8,128)S(1)}, f32[192,384]{1,0:T(8,128)S(1)}, u32[]{:S(2)}, u32[]{:S(2)}) %collective-permute-start.11) | collective-permute-done | bytes 294944 | tf_op jit(solution)/shard_map/ppermute | solution.py:316
  41.9 0.0 collective-permute-start.7
  41.9 0.1 shard_map.91.left
  42.0 0.2 shard_map.92.right
  42.3 0.0 collective-permute-done.12.one_b
  42.3 0.0 collective-permute-done.13.two_b
  42.3 2.2 %shard_map.100.rest_0_ = f32[2,384,384]{2,1,0:T(8,128)} custom-call(s32[1,2]{1,0:T(1,128)S(1)} %bitcast.11, f32[2,2]{1,0:T(2,128)S(1)} %copy-done.1, bf16[384,1152]{1,0:T(8,128)(2,1)S(1)} %shard_map.91.left, bf16[1152,384]{1,0:T(8,128)(2,1)S(1)} %shard_map.92.right, f32[192,384]{1,0:T(8,128)S(1)} %collective-permute-done.8.one_a, ...), custom_call_target="tpu_custom_call" | custom-call | flops 339738624 | bytes 6488088 | tf_op jit(solution)/shard_map/pallas_call | solution.py:292
  44.5 2.4 %collective-permute-done.5.across_a = f32[192,384]{1,0:T(8,128)S(1)} collective-permute-done((f32[192,384]{1,0:T(8,128)S(1)}, f32[192,384]{1,0:T(8,128)S(1)}, u32[]{:S(2)}, u32[]{:S(2)}) %collective-permute-start.5) | collective-permute-done | bytes 294944 | tf_op jit(solution)/shard_map/ppermute | solution.py:316
  46.9 0.0 collective-permute-done.6.one_b
  46.9 0.0 collective-permute-done.7.two_b
  46.9 2.2 %shard_map.101 = f32[2,384,384]{2,1,0:T(8,128)} custom-call(s32[1,2]{1,0:T(1,128)S(1)} %bitcast.12, f32[2,2]{1,0:T(2,128)S(1)} %copy-done.1, bf16[384,1152]{1,0:T(8,128)(2,1)S(1)} %shard_map.91.left, bf16[1152,384]{1,0:T(8,128)(2,1)S(1)} %shard_map.92.right, f32[192,384]{1,0:T(8,128)S(1)} %collective-permute-done.2.one_a, ...), custom_call_target="tpu_custom_call", output_to_operand_aliasing={{}: (10, {})} | custom-call | flops 339738624 | bytes 7667736 | tf_op jit(solution)/shard_map/pallas_call | solution.py:292
  (4 shorter events, 0.0 us)
Async XLA Ops:
  6.1 6.5 %collective-permute-start = (f32[128,256]{1,0:T(8,128)S(1)}, f32[128,256]{1,0:T(8,128)S(1)}, u32[]{:S(2)}, u32[]{:S(2)}) collective-permute-start(f32[128,256]{1,0:T(8,128)S(1)} %get-tuple-element.29), channel_id=1, source_target_pairs={{0,16},{8,24},{16,0},{24,8},{1,17},{9,25},{17,1},{25,9},{2,18},{10... | collective-permute-start | bytes 393224 | tf_op jit(solution)/shard_map/ppermute | solution.py:369
  12.7 1.7 %collective-permute-start.1 = (f32[128,256]{1,0:T(8,128)S(1)}, f32[128,256]{1,0:T(8,128)S(1)}, u32[]{:S(2)}, u32[]{:S(2)}) collective-permute-start(f32[128,256]{1,0:T(8,128)S(1)} %add.3.near), channel_id=1, source_target_pairs={{0,8},{8,0},{16,24},{24,16},{1,9},{9,1},{17,25},{25,17},{2,10},{10... | collective-permute-start | bytes 393224 | tf_op jit(solution)/shard_map/ppermute | solution.py:369
  12.8 1.6 %copy-start.3 = (f32[128,128]{1,0:T(8,128)S(1)}, f32[128,128]{1,0:T(8,128)}, u32[]{:S(2)}) copy-start(f32[128,128]{1,0:T(8,128)} %hamiltonian.1) | copy-start | bytes 196612
  12.8 1.6 %copy-start.4 = (f32[1,128]{1,0:T(1,128)S(1)}, f32[1,128]{1,0:T(1,128)}, u32[]{:S(2)}) copy-start(f32[1,128]{1,0:T(1,128)} %coupling.1) | copy-start | bytes 1540
  12.8 1.6 %copy-start.5 = (s32[1,128]{1,0:T(1,128)S(1)}, s32[1,128]{1,0:T(1,128)}, u32[]{:S(2)}) copy-start(s32[1,128]{1,0:T(1,128)} %bound.1) | copy-start | bytes 1540
  16.2 11.7 %copy-start.1 = (f32[2,2]{1,0:T(2,128)S(1)}, f32[2,2]{1,0:T(2,128)}, u32[]{:S(2)}) copy-start(f32[2,2]{1,0:T(2,128)} %weights.7) | copy-start | bytes 52
  16.2 11.7 %copy-start.2 = (s32[2]{0:T(128)S(1)}, s32[2]{0:T(128)}, u32[]{:S(2)}) copy-start(s32[2]{0:T(128)} %param.16) | copy-start | bytes 28
  16.3 9.5 %collective-permute-start.10 = (f32[192,384]{1,0:T(8,128)S(1)}, f32[192,384]{1,0:T(8,128)S(1)}, u32[]{:S(2)}, u32[]{:S(2)}) collective-permute-start(f32[192,384]{1,0:T(8,128)S(1)} %get-tuple-element.41.green_b), channel_id=1, source_target_pairs={{0,1},{1,0},{2,3},{3,2},{4,5},{5,4},{6,7},{7,6},{8,9},{9,8},{10,11... | collective-permute-start | bytes 884744 | tf_op jit(solution)/shard_map/ppermute | solution.py:316
  18.1 9.9 %collective-permute-start.8 = (f32[192,384]{1,0:T(8,128)S(1)}, f32[192,384]{1,0:T(8,128)S(1)}, u32[]{:S(2)}, u32[]{:S(2)}) collective-permute-start(f32[192,384]{1,0:T(8,128)S(1)} %get-tuple-element.40.green_a), channel_id=1, source_target_pairs={{0,2},{1,3},{2,0},{3,1},{4,6},{5,7},{6,4},{7,5},{8,10},{9,11},{10,... | collective-permute-start | bytes 884744 | tf_op jit(solution)/shard_map/ppermute | solution.py:316
  19.7 8.3 %collective-permute-start.9 = (f32[192,384]{1,0:T(8,128)S(1)}, f32[192,384]{1,0:T(8,128)S(1)}, u32[]{:S(2)}, u32[]{:S(2)}) collective-permute-start(f32[192,384]{1,0:T(8,128)S(1)} %get-tuple-element.40.green_a), channel_id=1, source_target_pairs={{0,8},{1,9},{2,4},{3,5},{4,2},{5,3},{6,14},{7,15},{8,0},{9,1},{10,... | collective-permute-start | bytes 884744 | tf_op jit(solution)/shard_map/ppermute | solution.py:316
  20.2 14.1 %collective-permute-start.2 = (f32[192,384]{1,0:T(8,128)S(1)}, f32[192,384]{1,0:T(8,128)S(1)}, u32[]{:S(2)}, u32[]{:S(2)}) collective-permute-start(f32[192,384]{1,0:T(8,128)S(1)} %get-tuple-element.35.green_a), channel_id=1, source_target_pairs={{0,2},{1,3},{2,0},{3,1},{4,6},{5,7},{6,4},{7,5},{8,10},{9,11},{10,... | collective-permute-start | bytes 884744 | tf_op jit(solution)/shard_map/ppermute | solution.py:316
  23.4 10.9 %collective-permute-start.3 = (f32[192,384]{1,0:T(8,128)S(1)}, f32[192,384]{1,0:T(8,128)S(1)}, u32[]{:S(2)}, u32[]{:S(2)}) collective-permute-start(f32[192,384]{1,0:T(8,128)S(1)} %get-tuple-element.35.green_a), channel_id=1, source_target_pairs={{0,8},{1,9},{2,4},{3,5},{4,2},{5,3},{6,14},{7,15},{8,0},{9,1},{10,... | collective-permute-start | bytes 884744 | tf_op jit(solution)/shard_map/ppermute | solution.py:316
  25.7 9.9 %collective-permute-start.4 = (f32[192,384]{1,0:T(8,128)S(1)}, f32[192,384]{1,0:T(8,128)S(1)}, u32[]{:S(2)}, u32[]{:S(2)}) collective-permute-start(f32[192,384]{1,0:T(8,128)S(1)} %get-tuple-element.36.green_b), channel_id=1, source_target_pairs={{0,1},{1,0},{2,3},{3,2},{4,5},{5,4},{6,7},{7,6},{8,9},{9,8},{10,11... | collective-permute-start | bytes 884744 | tf_op jit(solution)/shard_map/ppermute | solution.py:316
  28.0 13.9 %copy-start = (f32[1,384,384]{2,1,0:T(8,128)S(1)}, f32[1,384,384]{2,1,0:T(8,128)}, u32[]{:S(2)}) copy-start(f32[1,384,384]{2,1,0:T(8,128)} %param.15) | copy-start | bytes 1769476
  28.4 13.6 %collective-permute-start.11 = (f32[192,384]{1,0:T(8,128)S(1)}, f32[192,384]{1,0:T(8,128)S(1)}, u32[]{:S(2)}, u32[]{:S(2)}) collective-permute-start(f32[192,384]{1,0:T(8,128)S(1)} %get-tuple-element.42), channel_id=1, source_target_pairs={{0,1},{1,0},{2,3},{3,2},{4,5},{5,4},{6,7},{7,6},{8,9},{9,8},{10,11... | collective-permute-start | bytes 884744 | tf_op jit(solution)/shard_map/ppermute | solution.py:316
  28.7 13.6 %collective-permute-start.12 = (f32[192,384]{1,0:T(8,128)S(1)}, f32[192,384]{1,0:T(8,128)S(1)}, u32[]{:S(2)}, u32[]{:S(2)}) collective-permute-start(f32[192,384]{1,0:T(8,128)S(1)} %get-tuple-element.43), channel_id=1, source_target_pairs={{0,2},{1,3},{2,0},{3,1},{4,6},{5,7},{6,4},{7,5},{8,10},{9,11},{10,... | collective-permute-start | bytes 884744 | tf_op jit(solution)/shard_map/ppermute | solution.py:316
  34.3 8.0 %collective-permute-start.13 = (f32[192,384]{1,0:T(8,128)S(1)}, f32[192,384]{1,0:T(8,128)S(1)}, u32[]{:S(2)}, u32[]{:S(2)}) collective-permute-start(f32[192,384]{1,0:T(8,128)S(1)} %get-tuple-element.44), channel_id=1, source_target_pairs={{0,8},{1,9},{2,4},{3,5},{4,2},{5,3},{6,14},{7,15},{8,0},{9,1},{10,... | collective-permute-start | bytes 884744 | tf_op jit(solution)/shard_map/ppermute | solution.py:316
  36.0 10.9 %collective-permute-start.5 = (f32[192,384]{1,0:T(8,128)S(1)}, f32[192,384]{1,0:T(8,128)S(1)}, u32[]{:S(2)}, u32[]{:S(2)}) collective-permute-start(f32[192,384]{1,0:T(8,128)S(1)} %get-tuple-element.37), channel_id=1, source_target_pairs={{0,1},{1,0},{2,3},{3,2},{4,5},{5,4},{6,7},{7,6},{8,9},{9,8},{10,11... | collective-permute-start | bytes 884744 | tf_op jit(solution)/shard_map/ppermute | solution.py:316
  37.8 9.1 %collective-permute-start.6 = (f32[192,384]{1,0:T(8,128)S(1)}, f32[192,384]{1,0:T(8,128)S(1)}, u32[]{:S(2)}, u32[]{:S(2)}) collective-permute-start(f32[192,384]{1,0:T(8,128)S(1)} %get-tuple-element.38), channel_id=1, source_target_pairs={{0,2},{1,3},{2,0},{3,1},{4,6},{5,7},{6,4},{7,5},{8,10},{9,11},{10,... | collective-permute-start | bytes 884744 | tf_op jit(solution)/shard_map/ppermute | solution.py:316
  41.9 5.0 %collective-permute-start.7 = (f32[192,384]{1,0:T(8,128)S(1)}, f32[192,384]{1,0:T(8,128)S(1)}, u32[]{:S(2)}, u32[]{:S(2)}) collective-permute-start(f32[192,384]{1,0:T(8,128)S(1)} %get-tuple-element.39), channel_id=1, source_target_pairs={{0,8},{1,9},{2,4},{3,5},{4,2},{5,3},{6,14},{7,15},{8,0},{9,1},{10,... | collective-permute-start | bytes 884744 | tf_op jit(solution)/shard_map/ppermute | solution.py:316

commit v3 on v2

--- a/solution.py
+++ b/solution.py
@@ -116,8 +116,8 @@
         pltpu.make_async_copy(source, target, arrived.at[at])
         for at, (source, target) in enumerate(zip(sources, places))
     ]
-    for copy in copies:
-        copy.start()
+    for at in (2, 1, 0, 4, 3):
+        copies[at].start()
     for copy in copies:
         copy.wait()
     size, few = hopping.shape[0], coupling.shape[1]
@@ -150,17 +150,26 @@
     term[...] = jnp.concatenate([corner[:few], corner[few:]], axis=1)
 
 
-def power_kernel(first, second, start, partial, fourth):
+def power_kernel(first, second, start, partial, left, right):
     size = first.shape[0]
     one, two = first[...], second[...]
     both = dot(jnp.concatenate([left_of(one), left_of(two)], axis=0), right_of(two))
     total = unit(one.shape) + one + two + both[:size]
-    partial[...] = row_scaled((start[:, 0:1], start[:, 1:2]), total)
-    fourth[...] = both[size:]
-
-
-def slab_kernel(partial, fourth, inverse):
-    inverse[...] = partial[...] + product(partial[...], fourth[...])
+    total = row_scaled((start[:, 0:1], start[:, 1:2]), total)
+    partial[...] = total
+    left[...] = jnp.concatenate(split(total), axis=1)
+    high, low = split(both[size:])
+    for at, part in enumerate((high, turned(high), low, turned(low))):
+        right[at * size : (at + 1) * size] = part
+
+
+def slab_kernel(partial, left, right, inverse):
+    wide = partial.shape[1]
+    high, low = left[:, :wide], left[:, wide:]
+    inverse[...] = partial[...] + dot(
+        jnp.concatenate([high, high, low], axis=1),
+        jnp.concatenate([right[...], right[:wide]], axis=0),
+    )
 
 
 def columns_of(x, places):
@@ -360,15 +369,24 @@
         scratch_shapes=[pltpu.VMEM(x.shape, x.dtype) for x in given]
         + [pltpu.SemaphoreType.DMA((len(given),))],
     )
-    partial, fourth = call(power_kernel, [full, full], [first, second, start], flops=2 * cube)
+    partial, left_side, right_side = call(
+        power_kernel,
+        [
+            full,
+            jax.ShapeDtypeStruct((size, 4 * size), BF16),
+            jax.ShapeDtypeStruct((4 * size, 2 * size), BF16),
+        ],
+        [first, second, start],
+        flops=2 * cube,
+    )
     near, far, reach = term, None, slabs // 2
     while reach:
         if far is not None:
-            far, fourth = lax.optimization_barrier((far, fourth))
+            far, partial = lax.optimization_barrier((far, partial))
             near = near + far
         far = lax.ppermute(near, "slab", [(i, i ^ reach) for i in range(slabs)])
         reach //= 2
-    inverse = call(slab_kernel, full, [partial, fourth], flops=cube)
+    inverse = call(slab_kernel, full, [partial, left_side, right_side], flops=cube)
     part = held(half, size)
     middle, *greens = call(
         green_kernel,

time: 49.7 us -> 49.7 us (level)
  no operation moved by 1% of the time
where the time goes in v3:
time: 49.7 us; the launch traced here: 49 us
  Pallas kernels  18.5 us (37%)
  starting transfers between devices  18.2 us (37%)
  waiting for transfers between devices  12.1 us (24%)
    pallas_call x11, Pallas kernels, call(): pl.pallas_call(kernel, out_shape=outs, compiler_params=pltpu.CompilerPara...  18.5 us
    ppermute x12, starting transfers between devices, exchange(): return lax.ppermute(x, ('slab', 'energy'), pairs)  15.1 us
    ppermute x12, waiting for transfers between devices, exchange(): return lax.ppermute(x, ('slab', 'energy'), pairs)  11.8 us
    ppermute x2, starting transfers between devices, per_device(): far = lax.ppermute(near, 'slab', [(i, i ^ reach) for i in range(slabs)])  3.1 us
  transfers between devices with their start and end apart: 14, of which 7 were waited for; matrix products, arithmetic and copies ran while one was open for 0% of the time, Pallas kernels for 17%

profile of v3, /device:TPU:0, one launch (start us, length us, event | category | flops | bytes accessed | tf_op | source)
XLA Modules:
  0.0 49.0 jit_solution(15363951134456057958)
XLA Ops:
  0.0 6.1 %shard_map.93 = (f32[384,768]{1,0:T(8,128)S(1)}, f32[384,768]{1,0:T(8,128)S(1)}, f32[384,2]{1,0:T(8,128)S(1)}, f32[128,768]{1,0:T(8,128)S(1)}, f32[128,256]{1,0:T(8,128)S(1)}) custom-call(f32[1,384]{1,0:T(1,128)} %refs_0_.1, f32[384,384]{1,0:T(8,128)} %bitcast.14, f32[2,384,384]{2,1,0:T(8,128)} %bitcast.13, f32[1,128]{1,0:T(1,128)} %coupling.1, s32[1,128]{1,0:T(1,128)} %bound.1), custom_call_target="tpu_custom_call" | custom-call | flops 2717908992 | bytes 4658688 | tf_op jit(solution)/shard_map/pallas_call | solution.py:301
  6.1 3.0 %collective-permute-start = (f32[128,256]{1,0:T(8,128)S(1)}, f32[128,256]{1,0:T(8,128)S(1)}, u32[]{:S(2)}, u32[]{:S(2)}) collective-permute-start(f32[128,256]{1,0:T(8,128)S(1)} %get-tuple-element.26), channel_id=1, source_target_pairs={{0,16},{8,24},{16,0},{24,8},{1,17},{9,25},{17,1},{25,9},{2,18},{10... | collective-permute-start | bytes 393224 | tf_op jit(solution)/shard_map/ppermute | solution.py:387
  9.1 3.2 %shard_map.94 = (f32[384,768]{1,0:T(8,128)S(1)}, bf16[384,1536]{1,0:T(8,128)(2,1)S(1)}, bf16[1536,768]{1,0:T(8,128)(2,1)S(1)}) custom-call(f32[384,768]{1,0:T(8,128)S(1)} %get-tuple-element.27.first, f32[384,768]{1,0:T(8,128)S(1)} %get-tuple-element.28.second, f32[384,2]{1,0:T(8,128)S(1)} %get-tuple-element.29.start), custom_call_target="tpu_custom_call" | custom-call | flops 2717908992 | bytes 10619904 | tf_op jit(solution)/shard_map/pallas_call | solution.py:301
  12.3 0.3 collective-permute-done
  12.6 0.1 collective-permute-start.1
  12.7 0.0 copy-start.3
  12.7 0.0 copy-start.4
  12.7 0.0 copy-start.5
  12.7 1.5 %shard_map.95.inverse = f32[384,768]{1,0:T(8,128)S(1)} custom-call(f32[384,768]{1,0:T(8,128)S(1)} %get-tuple-element.31.partial, bf16[384,1536]{1,0:T(8,128)(2,1)S(1)} %get-tuple-element.32.left, bf16[1536,768]{1,0:T(8,128)(2,1)S(1)} %get-tuple-element.33.right), custom_call_target="tpu_custom_call" | custom-call | flops 1358954496 | bytes 9437184 | tf_op jit(solution)/shard_map/pallas_call | solution.py:301
  14.3 0.0 collective-permute-done.1.far
  14.3 0.0 copy-done.3
  14.3 0.0 copy-done.4
  14.3 1.8 %shard_map.96 = (f32[384,256]{1,0:T(8,128)S(1)}, f32[192,384]{1,0:T(8,128)S(1)}, f32[192,384]{1,0:T(8,128)S(1)}) custom-call(f32[128,128]{1,0:T(8,128)S(1)} %copy-done.3, f32[1,128]{1,0:T(1,128)S(1)} %copy-done.4, s32[1,128]{1,0:T(1,128)S(1)} %copy-done.5, f32[384,768]{1,0:T(8,128)S(1)} %shard_map.95.inverse, f32[128,768]{1,0:T(8,128)S(1)} %get-tuple-element.34.rows, ...), custom_call_target="tpu_custom_call" | custom-call | flops 1358954496 | bytes 2884608 | tf_op jit(solution)/shard_map/pallas_call | solution.py:301
  16.2 0.0 copy-start.1
  16.2 0.0 copy-start.2
  16.2 1.8 %collective-permute-start.10 = (f32[192,384]{1,0:T(8,128)S(1)}, f32[192,384]{1,0:T(8,128)S(1)}, u32[]{:S(2)}, u32[]{:S(2)}) collective-permute-start(f32[192,384]{1,0:T(8,128)S(1)} %get-tuple-element.43.green_b), channel_id=1, source_target_pairs={{0,1},{1,0},{2,3},{3,2},{4,5},{5,4},{6,7},{7,6},{8,9},{9,8},{10,11... | collective-permute-start | bytes 884744 | tf_op jit(solution)/shard_map/ppermute | solution.py:325
  18.0 1.6 %collective-permute-start.8 = (f32[192,384]{1,0:T(8,128)S(1)}, f32[192,384]{1,0:T(8,128)S(1)}, u32[]{:S(2)}, u32[]{:S(2)}) collective-permute-start(f32[192,384]{1,0:T(8,128)S(1)} %get-tuple-element.42.green_a), channel_id=1, source_target_pairs={{0,2},{1,3},{2,0},{3,1},{4,6},{5,7},{6,4},{7,5},{8,10},{9,11},{10,... | collective-permute-start | bytes 884744 | tf_op jit(solution)/shard_map/ppermute | solution.py:325
  19.6 0.0 collective-permute-start.9
  19.6 0.5 shard_map.97
  20.1 3.2 %collective-permute-start.2 = (f32[192,384]{1,0:T(8,128)S(1)}, f32[192,384]{1,0:T(8,128)S(1)}, u32[]{:S(2)}, u32[]{:S(2)}) collective-permute-start(f32[192,384]{1,0:T(8,128)S(1)} %get-tuple-element.37.green_a), channel_id=1, source_target_pairs={{0,2},{1,3},{2,0},{3,1},{4,6},{5,7},{6,4},{7,5},{8,10},{9,11},{10,... | collective-permute-start | bytes 884744 | tf_op jit(solution)/shard_map/ppermute | solution.py:325
  23.3 0.0 collective-permute-start.3
  23.3 2.3 %collective-permute-done.10.pair_b = f32[192,384]{1,0:T(8,128)S(1)} collective-permute-done((f32[192,384]{1,0:T(8,128)S(1)}, f32[192,384]{1,0:T(8,128)S(1)}, u32[]{:S(2)}, u32[]{:S(2)}) %collective-permute-start.10) | collective-permute-done | bytes 294944 | tf_op jit(solution)/shard_map/ppermute | solution.py:325
  25.7 1.7 %collective-permute-start.4 = (f32[192,384]{1,0:T(8,128)S(1)}, f32[192,384]{1,0:T(8,128)S(1)}, u32[]{:S(2)}, u32[]{:S(2)}) collective-permute-start(f32[192,384]{1,0:T(8,128)S(1)} %get-tuple-element.38.green_b), channel_id=1, source_target_pairs={{0,1},{1,0},{2,3},{3,2},{4,5},{5,4},{6,7},{7,6},{8,9},{9,8},{10,11... | collective-permute-start | bytes 884744 | tf_op jit(solution)/shard_map/ppermute | solution.py:325
  27.4 0.5 %collective-permute-done.8.one_a = f32[192,384]{1,0:T(8,128)S(1)} collective-permute-done((f32[192,384]{1,0:T(8,128)S(1)}, f32[192,384]{1,0:T(8,128)S(1)}, u32[]{:S(2)}, u32[]{:S(2)}) %collective-permute-start.8) | collective-permute-done | bytes 294944 | tf_op jit(solution)/shard_map/ppermute | solution.py:325
  27.9 0.0 collective-permute-done.9.two_a
  27.9 0.0 copy-done.2
  27.9 0.0 copy-start
  27.9 0.4 shard_map.99
  28.3 0.3 collective-permute-start.11
  28.6 3.0 %collective-permute-start.12 = (f32[192,384]{1,0:T(8,128)S(1)}, f32[192,384]{1,0:T(8,128)S(1)}, u32[]{:S(2)}, u32[]{:S(2)}) collective-permute-start(f32[192,384]{1,0:T(8,128)S(1)} %get-tuple-element.45), channel_id=1, source_target_pairs={{0,2},{1,3},{2,0},{3,1},{4,6},{5,7},{6,4},{7,5},{8,10},{9,11},{10,... | collective-permute-start | bytes 884744 | tf_op jit(solution)/shard_map/ppermute | solution.py:325
  31.6 2.7 %collective-permute-done.2.one_a = f32[192,384]{1,0:T(8,128)S(1)} collective-permute-done((f32[192,384]{1,0:T(8,128)S(1)}, f32[192,384]{1,0:T(8,128)S(1)}, u32[]{:S(2)}, u32[]{:S(2)}) %collective-permute-start.2) | collective-permute-done | bytes 294944 | tf_op jit(solution)/shard_map/ppermute | solution.py:325
  34.2 0.0 collective-permute-start.13
  34.2 0.0 collective-permute-done.3.two_a
  34.2 1.3 %collective-permute-done.4.pair_b = f32[192,384]{1,0:T(8,128)S(1)} collective-permute-done((f32[192,384]{1,0:T(8,128)S(1)}, f32[192,384]{1,0:T(8,128)S(1)}, u32[]{:S(2)}, u32[]{:S(2)}) %collective-permute-start.4) | collective-permute-done | bytes 294944 | tf_op jit(solution)/shard_map/ppermute | solution.py:325
  35.5 0.4 shard_map.98
  35.9 1.8 %collective-permute-start.5 = (f32[192,384]{1,0:T(8,128)S(1)}, f32[192,384]{1,0:T(8,128)S(1)}, u32[]{:S(2)}, u32[]{:S(2)}) collective-permute-start(f32[192,384]{1,0:T(8,128)S(1)} %get-tuple-element.39), channel_id=1, source_target_pairs={{0,1},{1,0},{2,3},{3,2},{4,5},{5,4},{6,7},{7,6},{8,9},{9,8},{10,11... | collective-permute-start | bytes 884744 | tf_op jit(solution)/shard_map/ppermute | solution.py:325
  37.7 1.6 %collective-permute-start.6 = (f32[192,384]{1,0:T(8,128)S(1)}, f32[192,384]{1,0:T(8,128)S(1)}, u32[]{:S(2)}, u32[]{:S(2)}) collective-permute-start(f32[192,384]{1,0:T(8,128)S(1)} %get-tuple-element.40), channel_id=1, source_target_pairs={{0,2},{1,3},{2,0},{3,1},{4,6},{5,7},{6,4},{7,5},{8,10},{9,11},{10,... | collective-permute-start | bytes 884744 | tf_op jit(solution)/shard_map/ppermute | solution.py:325
  39.3 2.6 %collective-permute-done.11.across_a = f32[192,384]{1,0:T(8,128)S(1)} collective-permute-done((f32[192,384]{1,0:T(8,128)S(1)}, f32[192,384]{1,0:T(8,128)S(1)}, u32[]{:S(2)}, u32[]{:S(2)}) %collective-permute-start.11) | collective-permute-done | bytes 294944 | tf_op jit(solution)/shard_map/ppermute | solution.py:325
  41.9 0.0 collective-permute-start.7
  41.9 0.1 shard_map.91.left
  42.0 0.2 shard_map.92.right
  42.2 0.0 collective-permute-done.12.one_b
  42.2 0.0 collective-permute-done.13.two_b
  42.2 2.2 %shard_map.100.rest_0_ = f32[2,384,384]{2,1,0:T(8,128)} custom-call(s32[1,2]{1,0:T(1,128)S(1)} %bitcast.11, f32[2,2]{1,0:T(2,128)S(1)} %copy-done.1, bf16[384,1152]{1,0:T(8,128)(2,1)S(1)} %shard_map.91.left, bf16[1152,384]{1,0:T(8,128)(2,1)S(1)} %shard_map.92.right, f32[192,384]{1,0:T(8,128)S(1)} %collective-permute-done.8.one_a, ...), custom_call_target="tpu_custom_call" | custom-call | flops 339738624 | bytes 6488088 | tf_op jit(solution)/shard_map/pallas_call | solution.py:301
  44.4 2.4 %collective-permute-done.5.across_a = f32[192,384]{1,0:T(8,128)S(1)} collective-permute-done((f32[192,384]{1,0:T(8,128)S(1)}, f32[192,384]{1,0:T(8,128)S(1)}, u32[]{:S(2)}, u32[]{:S(2)}) %collective-permute-start.5) | collective-permute-done | bytes 294944 | tf_op jit(solution)/shard_map/ppermute | solution.py:325
  46.8 0.0 collective-permute-done.6.one_b
  46.8 0.0 collective-permute-done.7.two_b
  46.9 2.2 %shard_map.101 = f32[2,384,384]{2,1,0:T(8,128)} custom-call(s32[1,2]{1,0:T(1,128)S(1)} %bitcast.12, f32[2,2]{1,0:T(2,128)S(1)} %copy-done.1, bf16[384,1152]{1,0:T(8,128)(2,1)S(1)} %shard_map.91.left, bf16[1152,384]{1,0:T(8,128)(2,1)S(1)} %shard_map.92.right, f32[192,384]{1,0:T(8,128)S(1)} %collective-permute-done.2.one_a, ...), custom_call_target="tpu_custom_call", output_to_operand_aliasing={{}: (10, {})} | custom-call | flops 339738624 | bytes 7667736 | tf_op jit(solution)/shard_map/pallas_call | solution.py:301
  (4 shorter events, 0.0 us)
Async XLA Ops:
  6.1 6.5 %collective-permute-start = (f32[128,256]{1,0:T(8,128)S(1)}, f32[128,256]{1,0:T(8,128)S(1)}, u32[]{:S(2)}, u32[]{:S(2)}) collective-permute-start(f32[128,256]{1,0:T(8,128)S(1)} %get-tuple-element.26), channel_id=1, source_target_pairs={{0,16},{8,24},{16,0},{24,8},{1,17},{9,25},{17,1},{25,9},{2,18},{10... | collective-permute-start | bytes 393224 | tf_op jit(solution)/shard_map/ppermute | solution.py:387
  12.6 1.7 %collective-permute-start.1 = (f32[128,256]{1,0:T(8,128)S(1)}, f32[128,256]{1,0:T(8,128)S(1)}, u32[]{:S(2)}, u32[]{:S(2)}) collective-permute-start(f32[128,256]{1,0:T(8,128)S(1)} %add.3.near), channel_id=1, source_target_pairs={{0,8},{8,0},{16,24},{24,16},{1,9},{9,1},{17,25},{25,17},{2,10},{10... | collective-permute-start | bytes 393224 | tf_op jit(solution)/shard_map/ppermute | solution.py:387
  12.7 1.6 %copy-start.3 = (f32[128,128]{1,0:T(8,128)S(1)}, f32[128,128]{1,0:T(8,128)}, u32[]{:S(2)}) copy-start(f32[128,128]{1,0:T(8,128)} %hamiltonian.1) | copy-start | bytes 196612
  12.7 1.6 %copy-start.4 = (f32[1,128]{1,0:T(1,128)S(1)}, f32[1,128]{1,0:T(1,128)}, u32[]{:S(2)}) copy-start(f32[1,128]{1,0:T(1,128)} %coupling.1) | copy-start | bytes 1540
  12.7 1.6 %copy-start.5 = (s32[1,128]{1,0:T(1,128)S(1)}, s32[1,128]{1,0:T(1,128)}, u32[]{:S(2)}) copy-start(s32[1,128]{1,0:T(1,128)} %bound.1) | copy-start | bytes 1540
  16.2 11.8 %copy-start.1 = (f32[2,2]{1,0:T(2,128)S(1)}, f32[2,2]{1,0:T(2,128)}, u32[]{:S(2)}) copy-start(f32[2,2]{1,0:T(2,128)} %weights.7) | copy-start | bytes 52
  16.2 11.7 %copy-start.2 = (s32[2]{0:T(128)S(1)}, s32[2]{0:T(128)}, u32[]{:S(2)}) copy-start(s32[2]{0:T(128)} %param.16) | copy-start | bytes 28
  16.2 9.5 %collective-permute-start.10 = (f32[192,384]{1,0:T(8,128)S(1)}, f32[192,384]{1,0:T(8,128)S(1)}, u32[]{:S(2)}, u32[]{:S(2)}) collective-permute-start(f32[192,384]{1,0:T(8,128)S(1)} %get-tuple-element.43.green_b), channel_id=1, source_target_pairs={{0,1},{1,0},{2,3},{3,2},{4,5},{5,4},{6,7},{7,6},{8,9},{9,8},{10,11... | collective-permute-start | bytes 884744 | tf_op jit(solution)/shard_map/ppermute | solution.py:325
  18.0 9.9 %collective-permute-start.8 = (f32[192,384]{1,0:T(8,128)S(1)}, f32[192,384]{1,0:T(8,128)S(1)}, u32[]{:S(2)}, u32[]{:S(2)}) collective-permute-start(f32[192,384]{1,0:T(8,128)S(1)} %get-tuple-element.42.green_a), channel_id=1, source_target_pairs={{0,2},{1,3},{2,0},{3,1},{4,6},{5,7},{6,4},{7,5},{8,10},{9,11},{10,... | collective-permute-start | bytes 884744 | tf_op jit(solution)/shard_map/ppermute | solution.py:325
  19.6 8.3 %collective-permute-start.9 = (f32[192,384]{1,0:T(8,128)S(1)}, f32[192,384]{1,0:T(8,128)S(1)}, u32[]{:S(2)}, u32[]{:S(2)}) collective-permute-start(f32[192,384]{1,0:T(8,128)S(1)} %get-tuple-element.42.green_a), channel_id=1, source_target_pairs={{0,8},{1,9},{2,4},{3,5},{4,2},{5,3},{6,14},{7,15},{8,0},{9,1},{10,... | collective-permute-start | bytes 884744 | tf_op jit(solution)/shard_map/ppermute | solution.py:325
  20.1 14.1 %collective-permute-start.2 = (f32[192,384]{1,0:T(8,128)S(1)}, f32[192,384]{1,0:T(8,128)S(1)}, u32[]{:S(2)}, u32[]{:S(2)}) collective-permute-start(f32[192,384]{1,0:T(8,128)S(1)} %get-tuple-element.37.green_a), channel_id=1, source_target_pairs={{0,2},{1,3},{2,0},{3,1},{4,6},{5,7},{6,4},{7,5},{8,10},{9,11},{10,... | collective-permute-start | bytes 884744 | tf_op jit(solution)/shard_map/ppermute | solution.py:325
  23.3 10.9 %collective-permute-start.3 = (f32[192,384]{1,0:T(8,128)S(1)}, f32[192,384]{1,0:T(8,128)S(1)}, u32[]{:S(2)}, u32[]{:S(2)}) collective-permute-start(f32[192,384]{1,0:T(8,128)S(1)} %get-tuple-element.37.green_a), channel_id=1, source_target_pairs={{0,8},{1,9},{2,4},{3,5},{4,2},{5,3},{6,14},{7,15},{8,0},{9,1},{10,... | collective-permute-start | bytes 884744 | tf_op jit(solution)/shard_map/ppermute | solution.py:325
  25.7 9.9 %collective-permute-start.4 = (f32[192,384]{1,0:T(8,128)S(1)}, f32[192,384]{1,0:T(8,128)S(1)}, u32[]{:S(2)}, u32[]{:S(2)}) collective-permute-start(f32[192,384]{1,0:T(8,128)S(1)} %get-tuple-element.38.green_b), channel_id=1, source_target_pairs={{0,1},{1,0},{2,3},{3,2},{4,5},{5,4},{6,7},{7,6},{8,9},{9,8},{10,11... | collective-permute-start | bytes 884744 | tf_op jit(solution)/shard_map/ppermute | solution.py:325
  27.9 13.9 %copy-start = (f32[1,384,384]{2,1,0:T(8,128)S(1)}, f32[1,384,384]{2,1,0:T(8,128)}, u32[]{:S(2)}) copy-start(f32[1,384,384]{2,1,0:T(8,128)} %param.15) | copy-start | bytes 1769476
  28.3 13.6 %collective-permute-start.11 = (f32[192,384]{1,0:T(8,128)S(1)}, f32[192,384]{1,0:T(8,128)S(1)}, u32[]{:S(2)}, u32[]{:S(2)}) collective-permute-start(f32[192,384]{1,0:T(8,128)S(1)} %get-tuple-element.44), channel_id=1, source_target_pairs={{0,1},{1,0},{2,3},{3,2},{4,5},{5,4},{6,7},{7,6},{8,9},{9,8},{10,11... | collective-permute-start | bytes 884744 | tf_op jit(solution)/shard_map/ppermute | solution.py:325
  28.6 13.6 %collective-permute-start.12 = (f32[192,384]{1,0:T(8,128)S(1)}, f32[192,384]{1,0:T(8,128)S(1)}, u32[]{:S(2)}, u32[]{:S(2)}) collective-permute-start(f32[192,384]{1,0:T(8,128)S(1)} %get-tuple-element.45), channel_id=1, source_target_pairs={{0,2},{1,3},{2,0},{3,1},{4,6},{5,7},{6,4},{7,5},{8,10},{9,11},{10,... | collective-permute-start | bytes 884744 | tf_op jit(solution)/shard_map/ppermute | solution.py:325
  34.2 8.0 %collective-permute-start.13 = (f32[192,384]{1,0:T(8,128)S(1)}, f32[192,384]{1,0:T(8,128)S(1)}, u32[]{:S(2)}, u32[]{:S(2)}) collective-permute-start(f32[192,384]{1,0:T(8,128)S(1)} %get-tuple-element.46), channel_id=1, source_target_pairs={{0,8},{1,9},{2,4},{3,5},{4,2},{5,3},{6,14},{7,15},{8,0},{9,1},{10,... | collective-permute-start | bytes 884744 | tf_op jit(solution)/shard_map/ppermute | solution.py:325
  35.9 10.9 %collective-permute-start.5 = (f32[192,384]{1,0:T(8,128)S(1)}, f32[192,384]{1,0:T(8,128)S(1)}, u32[]{:S(2)}, u32[]{:S(2)}) collective-permute-start(f32[192,384]{1,0:T(8,128)S(1)} %get-tuple-element.39), channel_id=1, source_target_pairs={{0,1},{1,0},{2,3},{3,2},{4,5},{5,4},{6,7},{7,6},{8,9},{9,8},{10,11... | collective-permute-start | bytes 884744 | tf_op jit(solution)/shard_map/ppermute | solution.py:325
  37.7 9.1 %collective-permute-start.6 = (f32[192,384]{1,0:T(8,128)S(1)}, f32[192,384]{1,0:T(8,128)S(1)}, u32[]{:S(2)}, u32[]{:S(2)}) collective-permute-start(f32[192,384]{1,0:T(8,128)S(1)} %get-tuple-element.40), channel_id=1, source_target_pairs={{0,2},{1,3},{2,0},{3,1},{4,6},{5,7},{6,4},{7,5},{8,10},{9,11},{10,... | collective-permute-start | bytes 884744 | tf_op jit(solution)/shard_map/ppermute | solution.py:325
  41.9 5.0 %collective-permute-start.7 = (f32[192,384]{1,0:T(8,128)S(1)}, f32[192,384]{1,0:T(8,128)S(1)}, u32[]{:S(2)}, u32[]{:S(2)}) collective-permute-start(f32[192,384]{1,0:T(8,128)S(1)} %get-tuple-element.41), channel_id=1, source_target_pairs={{0,8},{1,9},{2,4},{3,5},{4,2},{5,3},{6,14},{7,15},{8,0},{9,1},{10,... | collective-permute-start | bytes 884744 | tf_op jit(solution)/shard_map/ppermute | solution.py:325

commit v4 on v3

--- a/solution.py
+++ b/solution.py
@@ -267,11 +267,12 @@
     high, low = split(jnp.concatenate([mixed_a, mixed_b], axis=0))
     high, low = split(dot(left[...], jnp.concatenate([high, low, high], axis=0)))
     outer = jnp.concatenate([high, high, low], axis=1)
-    half = mixed_a.shape[0]
+    size = left.shape[0]
+    cut = size * 2 // 3 // 16 * 16
     copies = []
-    for piece in (0, 1):
-        rows = pl.ds(piece * half, half)
-        held_out[rows] = dot(outer[piece * half : piece * half + half], right[...])
+    for piece, (row, count) in enumerate(((0, cut), (cut, size - cut))):
+        rows = pl.ds(row, count)
+        held_out[rows] = dot(outer[row : row + count], right[...])
         copies.append(pltpu.make_async_copy(held_out.at[rows], out.at[at, rows], sent.at[piece]))
         copies[-1].start()
     for copy in copies:

time: 49.7 us -> 49.6 us (level)
  no operation moved by 1% of the time
where the time goes in v4:
time: 49.6 us; the launch traced here: 49 us
  Pallas kernels  18.5 us (37%)
  starting transfers between devices  18.2 us (37%)
  waiting for transfers between devices  12.1 us (24%)
    pallas_call x11, Pallas kernels, call(): pl.pallas_call(kernel, out_shape=outs, compiler_params=pltpu.CompilerPara...  18.5 us
    ppermute x12, starting transfers between devices, exchange(): return lax.ppermute(x, ('slab', 'energy'), pairs)  15.1 us
    ppermute x12, waiting for transfers between devices, exchange(): return lax.ppermute(x, ('slab', 'energy'), pairs)  11.8 us
    ppermute x2, starting transfers between devices, per_device(): far = lax.ppermute(near, 'slab', [(i, i ^ reach) for i in range(slabs)])  3.1 us
  transfers between devices with their start and end apart: 14, of which 7 were waited for; matrix products, arithmetic and copies ran while one was open for 0% of the time, Pallas kernels for 17%

profile of v4, /device:TPU:0, one launch (start us, length us, event | category | flops | bytes accessed | tf_op | source)
XLA Modules:
  0.0 49.0 jit_solution(2350303039797920778)
XLA Ops:
  0.0 6.1 %shard_map.93 = (f32[384,768]{1,0:T(8,128)S(1)}, f32[384,768]{1,0:T(8,128)S(1)}, f32[384,2]{1,0:T(8,128)S(1)}, f32[128,768]{1,0:T(8,128)S(1)}, f32[128,256]{1,0:T(8,128)S(1)}) custom-call(f32[1,384]{1,0:T(1,128)} %refs_0_.1, f32[384,384]{1,0:T(8,128)} %bitcast.14, f32[2,384,384]{2,1,0:T(8,128)} %bitcast.13, f32[1,128]{1,0:T(1,128)} %coupling.1, s32[1,128]{1,0:T(1,128)} %bound.1), custom_call_target="tpu_custom_call" | custom-call | flops 2717908992 | bytes 4658688 | tf_op jit(solution)/shard_map/pallas_call | solution.py:302
  6.1 3.0 %collective-permute-start = (f32[128,256]{1,0:T(8,128)S(1)}, f32[128,256]{1,0:T(8,128)S(1)}, u32[]{:S(2)}, u32[]{:S(2)}) collective-permute-start(f32[128,256]{1,0:T(8,128)S(1)} %get-tuple-element.26), channel_id=1, source_target_pairs={{0,16},{8,24},{16,0},{24,8},{1,17},{9,25},{17,1},{25,9},{2,18},{10... | collective-permute-start | bytes 393224 | tf_op jit(solution)/shard_map/ppermute | solution.py:388
  9.1 3.2 %shard_map.94 = (f32[384,768]{1,0:T(8,128)S(1)}, bf16[384,1536]{1,0:T(8,128)(2,1)S(1)}, bf16[1536,768]{1,0:T(8,128)(2,1)S(1)}) custom-call(f32[384,768]{1,0:T(8,128)S(1)} %get-tuple-element.27.first, f32[384,768]{1,0:T(8,128)S(1)} %get-tuple-element.28.second, f32[384,2]{1,0:T(8,128)S(1)} %get-tuple-element.29.start), custom_call_target="tpu_custom_call" | custom-call | flops 2717908992 | bytes 10619904 | tf_op jit(solution)/shard_map/pallas_call | solution.py:302
  12.3 0.3 collective-permute-done
  12.6 0.1 collective-permute-start.1
  12.7 0.0 copy-start.3
  12.7 0.0 copy-start.4
  12.7 0.0 copy-start.5
  12.7 1.5 %shard_map.95.inverse = f32[384,768]{1,0:T(8,128)S(1)} custom-call(f32[384,768]{1,0:T(8,128)S(1)} %get-tuple-element.31.partial, bf16[384,1536]{1,0:T(8,128)(2,1)S(1)} %get-tuple-element.32.left, bf16[1536,768]{1,0:T(8,128)(2,1)S(1)} %get-tuple-element.33.right), custom_call_target="tpu_custom_call" | custom-call | flops 1358954496 | bytes 9437184 | tf_op jit(solution)/shard_map/pallas_call | solution.py:302
  14.3 0.0 collective-permute-done.1.far
  14.3 0.0 copy-done.3
  14.3 0.0 copy-done.4
  14.3 1.8 %shard_map.96 = (f32[384,256]{1,0:T(8,128)S(1)}, f32[192,384]{1,0:T(8,128)S(1)}, f32[192,384]{1,0:T(8,128)S(1)}) custom-call(f32[128,128]{1,0:T(8,128)S(1)} %copy-done.3, f32[1,128]{1,0:T(1,128)S(1)} %copy-done.4, s32[1,128]{1,0:T(1,128)S(1)} %copy-done.5, f32[384,768]{1,0:T(8,128)S(1)} %shard_map.95.inverse, f32[128,768]{1,0:T(8,128)S(1)} %get-tuple-element.34.rows, ...), custom_call_target="tpu_custom_call" | custom-call | flops 1358954496 | bytes 2884608 | tf_op jit(solution)/shard_map/pallas_call | solution.py:302
  16.2 0.0 copy-start.1
  16.2 0.0 copy-start.2
  16.2 1.8 %collective-permute-start.10 = (f32[192,384]{1,0:T(8,128)S(1)}, f32[192,384]{1,0:T(8,128)S(1)}, u32[]{:S(2)}, u32[]{:S(2)}) collective-permute-start(f32[192,384]{1,0:T(8,128)S(1)} %get-tuple-element.43.green_b), channel_id=1, source_target_pairs={{0,1},{1,0},{2,3},{3,2},{4,5},{5,4},{6,7},{7,6},{8,9},{9,8},{10,11... | collective-permute-start | bytes 884744 | tf_op jit(solution)/shard_map/ppermute | solution.py:326
  18.0 1.6 %collective-permute-start.8 = (f32[192,384]{1,0:T(8,128)S(1)}, f32[192,384]{1,0:T(8,128)S(1)}, u32[]{:S(2)}, u32[]{:S(2)}) collective-permute-start(f32[192,384]{1,0:T(8,128)S(1)} %get-tuple-element.42.green_a), channel_id=1, source_target_pairs={{0,2},{1,3},{2,0},{3,1},{4,6},{5,7},{6,4},{7,5},{8,10},{9,11},{10,... | collective-permute-start | bytes 884744 | tf_op jit(solution)/shard_map/ppermute | solution.py:326
  19.6 0.0 collective-permute-start.9
  19.6 0.5 shard_map.97
  20.1 3.2 %collective-permute-start.2 = (f32[192,384]{1,0:T(8,128)S(1)}, f32[192,384]{1,0:T(8,128)S(1)}, u32[]{:S(2)}, u32[]{:S(2)}) collective-permute-start(f32[192,384]{1,0:T(8,128)S(1)} %get-tuple-element.37.green_a), channel_id=1, source_target_pairs={{0,2},{1,3},{2,0},{3,1},{4,6},{5,7},{6,4},{7,5},{8,10},{9,11},{10,... | collective-permute-start | bytes 884744 | tf_op jit(solution)/shard_map/ppermute | solution.py:326
  23.3 0.0 collective-permute-start.3
  23.3 2.3 %collective-permute-done.10.pair_b = f32[192,384]{1,0:T(8,128)S(1)} collective-permute-done((f32[192,384]{1,0:T(8,128)S(1)}, f32[192,384]{1,0:T(8,128)S(1)}, u32[]{:S(2)}, u32[]{:S(2)}) %collective-permute-start.10) | collective-permute-done | bytes 294944 | tf_op jit(solution)/shard_map/ppermute | solution.py:326
  25.7 1.7 %collective-permute-start.4 = (f32[192,384]{1,0:T(8,128)S(1)}, f32[192,384]{1,0:T(8,128)S(1)}, u32[]{:S(2)}, u32[]{:S(2)}) collective-permute-start(f32[192,384]{1,0:T(8,128)S(1)} %get-tuple-element.38.green_b), channel_id=1, source_target_pairs={{0,1},{1,0},{2,3},{3,2},{4,5},{5,4},{6,7},{7,6},{8,9},{9,8},{10,11... | collective-permute-start | bytes 884744 | tf_op jit(solution)/shard_map/ppermute | solution.py:326
  27.4 0.5 %collective-permute-done.8.one_a = f32[192,384]{1,0:T(8,128)S(1)} collective-permute-done((f32[192,384]{1,0:T(8,128)S(1)}, f32[192,384]{1,0:T(8,128)S(1)}, u32[]{:S(2)}, u32[]{:S(2)}) %collective-permute-start.8) | collective-permute-done | bytes 294944 | tf_op jit(solution)/shard_map/ppermute | solution.py:326
  27.9 0.0 collective-permute-done.9.two_a
  27.9 0.0 copy-done.2
  27.9 0.0 copy-start
  27.9 0.4 shard_map.99
  28.3 0.3 collective-permute-start.11
  28.6 3.0 %collective-permute-start.12 = (f32[192,384]{1,0:T(8,128)S(1)}, f32[192,384]{1,0:T(8,128)S(1)}, u32[]{:S(2)}, u32[]{:S(2)}) collective-permute-start(f32[192,384]{1,0:T(8,128)S(1)} %get-tuple-element.45), channel_id=1, source_target_pairs={{0,2},{1,3},{2,0},{3,1},{4,6},{5,7},{6,4},{7,5},{8,10},{9,11},{10,... | collective-permute-start | bytes 884744 | tf_op jit(solution)/shard_map/ppermute | solution.py:326
  31.6 2.7 %collective-permute-done.2.one_a = f32[192,384]{1,0:T(8,128)S(1)} collective-permute-done((f32[192,384]{1,0:T(8,128)S(1)}, f32[192,384]{1,0:T(8,128)S(1)}, u32[]{:S(2)}, u32[]{:S(2)}) %collective-permute-start.2) | collective-permute-done | bytes 294944 | tf_op jit(solution)/shard_map/ppermute | solution.py:326
  34.2 0.0 collective-permute-start.13
  34.2 0.0 collective-permute-done.3.two_a
  34.2 1.3 %collective-permute-done.4.pair_b = f32[192,384]{1,0:T(8,128)S(1)} collective-permute-done((f32[192,384]{1,0:T(8,128)S(1)}, f32[192,384]{1,0:T(8,128)S(1)}, u32[]{:S(2)}, u32[]{:S(2)}) %collective-permute-start.4) | collective-permute-done | bytes 294944 | tf_op jit(solution)/shard_map/ppermute | solution.py:326
  35.5 0.4 shard_map.98
  35.9 1.8 %collective-permute-start.5 = (f32[192,384]{1,0:T(8,128)S(1)}, f32[192,384]{1,0:T(8,128)S(1)}, u32[]{:S(2)}, u32[]{:S(2)}) collective-permute-start(f32[192,384]{1,0:T(8,128)S(1)} %get-tuple-element.39), channel_id=1, source_target_pairs={{0,1},{1,0},{2,3},{3,2},{4,5},{5,4},{6,7},{7,6},{8,9},{9,8},{10,11... | collective-permute-start | bytes 884744 | tf_op jit(solution)/shard_map/ppermute | solution.py:326
  37.7 1.6 %collective-permute-start.6 = (f32[192,384]{1,0:T(8,128)S(1)}, f32[192,384]{1,0:T(8,128)S(1)}, u32[]{:S(2)}, u32[]{:S(2)}) collective-permute-start(f32[192,384]{1,0:T(8,128)S(1)} %get-tuple-element.40), channel_id=1, source_target_pairs={{0,2},{1,3},{2,0},{3,1},{4,6},{5,7},{6,4},{7,5},{8,10},{9,11},{10,... | collective-permute-start | bytes 884744 | tf_op jit(solution)/shard_map/ppermute | solution.py:326
  39.3 2.6 %collective-permute-done.11.across_a = f32[192,384]{1,0:T(8,128)S(1)} collective-permute-done((f32[192,384]{1,0:T(8,128)S(1)}, f32[192,384]{1,0:T(8,128)S(1)}, u32[]{:S(2)}, u32[]{:S(2)}) %collective-permute-start.11) | collective-permute-done | bytes 294944 | tf_op jit(solution)/shard_map/ppermute | solution.py:326
  41.9 0.0 collective-permute-start.7
  41.9 0.1 shard_map.91.left
  42.0 0.2 shard_map.92.right
  42.2 0.0 collective-permute-done.12.one_b
  42.2 0.0 collective-permute-done.13.two_b
  42.2 2.2 %shard_map.100.rest_0_ = f32[2,384,384]{2,1,0:T(8,128)} custom-call(s32[1,2]{1,0:T(1,128)S(1)} %bitcast.11, f32[2,2]{1,0:T(2,128)S(1)} %copy-done.1, bf16[384,1152]{1,0:T(8,128)(2,1)S(1)} %shard_map.91.left, bf16[1152,384]{1,0:T(8,128)(2,1)S(1)} %shard_map.92.right, f32[192,384]{1,0:T(8,128)S(1)} %collective-permute-done.8.one_a, ...), custom_call_target="tpu_custom_call" | custom-call | flops 339738624 | bytes 6488088 | tf_op jit(solution)/shard_map/pallas_call | solution.py:302
  44.4 2.5 %collective-permute-done.5.across_a = f32[192,384]{1,0:T(8,128)S(1)} collective-permute-done((f32[192,384]{1,0:T(8,128)S(1)}, f32[192,384]{1,0:T(8,128)S(1)}, u32[]{:S(2)}, u32[]{:S(2)}) %collective-permute-start.5) | collective-permute-done | bytes 294944 | tf_op jit(solution)/shard_map/ppermute | solution.py:326
  46.8 0.0 collective-permute-done.6.one_b
  46.8 0.0 collective-permute-done.7.two_b
  46.9 2.2 %shard_map.101 = f32[2,384,384]{2,1,0:T(8,128)} custom-call(s32[1,2]{1,0:T(1,128)S(1)} %bitcast.12, f32[2,2]{1,0:T(2,128)S(1)} %copy-done.1, bf16[384,1152]{1,0:T(8,128)(2,1)S(1)} %shard_map.91.left, bf16[1152,384]{1,0:T(8,128)(2,1)S(1)} %shard_map.92.right, f32[192,384]{1,0:T(8,128)S(1)} %collective-permute-done.2.one_a, ...), custom_call_target="tpu_custom_call", output_to_operand_aliasing={{}: (10, {})} | custom-call | flops 339738624 | bytes 7667736 | tf_op jit(solution)/shard_map/pallas_call | solution.py:302
  (4 shorter events, 0.0 us)
Async XLA Ops:
  6.1 6.5 %collective-permute-start = (f32[128,256]{1,0:T(8,128)S(1)}, f32[128,256]{1,0:T(8,128)S(1)}, u32[]{:S(2)}, u32[]{:S(2)}) collective-permute-start(f32[128,256]{1,0:T(8,128)S(1)} %get-tuple-element.26), channel_id=1, source_target_pairs={{0,16},{8,24},{16,0},{24,8},{1,17},{9,25},{17,1},{25,9},{2,18},{10... | collective-permute-start | bytes 393224 | tf_op jit(solution)/shard_map/ppermute | solution.py:388
  12.6 1.7 %collective-permute-start.1 = (f32[128,256]{1,0:T(8,128)S(1)}, f32[128,256]{1,0:T(8,128)S(1)}, u32[]{:S(2)}, u32[]{:S(2)}) collective-permute-start(f32[128,256]{1,0:T(8,128)S(1)} %add.3.near), channel_id=1, source_target_pairs={{0,8},{8,0},{16,24},{24,16},{1,9},{9,1},{17,25},{25,17},{2,10},{10... | collective-permute-start | bytes 393224 | tf_op jit(solution)/shard_map/ppermute | solution.py:388
  12.7 1.6 %copy-start.3 = (f32[128,128]{1,0:T(8,128)S(1)}, f32[128,128]{1,0:T(8,128)}, u32[]{:S(2)}) copy-start(f32[128,128]{1,0:T(8,128)} %hamiltonian.1) | copy-start | bytes 196612
  12.7 1.6 %copy-start.4 = (f32[1,128]{1,0:T(1,128)S(1)}, f32[1,128]{1,0:T(1,128)}, u32[]{:S(2)}) copy-start(f32[1,128]{1,0:T(1,128)} %coupling.1) | copy-start | bytes 1540
  12.7 1.6 %copy-start.5 = (s32[1,128]{1,0:T(1,128)S(1)}, s32[1,128]{1,0:T(1,128)}, u32[]{:S(2)}) copy-start(s32[1,128]{1,0:T(1,128)} %bound.1) | copy-start | bytes 1540
  16.2 11.8 %copy-start.1 = (f32[2,2]{1,0:T(2,128)S(1)}, f32[2,2]{1,0:T(2,128)}, u32[]{:S(2)}) copy-start(f32[2,2]{1,0:T(2,128)} %weights.7) | copy-start | bytes 52
  16.2 11.7 %copy-start.2 = (s32[2]{0:T(128)S(1)}, s32[2]{0:T(128)}, u32[]{:S(2)}) copy-start(s32[2]{0:T(128)} %param.16) | copy-start | bytes 28
  16.2 9.5 %collective-permute-start.10 = (f32[192,384]{1,0:T(8,128)S(1)}, f32[192,384]{1,0:T(8,128)S(1)}, u32[]{:S(2)}, u32[]{:S(2)}) collective-permute-start(f32[192,384]{1,0:T(8,128)S(1)} %get-tuple-element.43.green_b), channel_id=1, source_target_pairs={{0,1},{1,0},{2,3},{3,2},{4,5},{5,4},{6,7},{7,6},{8,9},{9,8},{10,11... | collective-permute-start | bytes 884744 | tf_op jit(solution)/shard_map/ppermute | solution.py:326
  18.0 9.9 %collective-permute-start.8 = (f32[192,384]{1,0:T(8,128)S(1)}, f32[192,384]{1,0:T(8,128)S(1)}, u32[]{:S(2)}, u32[]{:S(2)}) collective-permute-start(f32[192,384]{1,0:T(8,128)S(1)} %get-tuple-element.42.green_a), channel_id=1, source_target_pairs={{0,2},{1,3},{2,0},{3,1},{4,6},{5,7},{6,4},{7,5},{8,10},{9,11},{10,... | collective-permute-start | bytes 884744 | tf_op jit(solution)/shard_map/ppermute | solution.py:326
  19.6 8.3 %collective-permute-start.9 = (f32[192,384]{1,0:T(8,128)S(1)}, f32[192,384]{1,0:T(8,128)S(1)}, u32[]{:S(2)}, u32[]{:S(2)}) collective-permute-start(f32[192,384]{1,0:T(8,128)S(1)} %get-tuple-element.42.green_a), channel_id=1, source_target_pairs={{0,8},{1,9},{2,4},{3,5},{4,2},{5,3},{6,14},{7,15},{8,0},{9,1},{10,... | collective-permute-start | bytes 884744 | tf_op jit(solution)/shard_map/ppermute | solution.py:326
  20.1 14.1 %collective-permute-start.2 = (f32[192,384]{1,0:T(8,128)S(1)}, f32[192,384]{1,0:T(8,128)S(1)}, u32[]{:S(2)}, u32[]{:S(2)}) collective-permute-start(f32[192,384]{1,0:T(8,128)S(1)} %get-tuple-element.37.green_a), channel_id=1, source_target_pairs={{0,2},{1,3},{2,0},{3,1},{4,6},{5,7},{6,4},{7,5},{8,10},{9,11},{10,... | collective-permute-start | bytes 884744 | tf_op jit(solution)/shard_map/ppermute | solution.py:326
  23.3 10.9 %collective-permute-start.3 = (f32[192,384]{1,0:T(8,128)S(1)}, f32[192,384]{1,0:T(8,128)S(1)}, u32[]{:S(2)}, u32[]{:S(2)}) collective-permute-start(f32[192,384]{1,0:T(8,128)S(1)} %get-tuple-element.37.green_a), channel_id=1, source_target_pairs={{0,8},{1,9},{2,4},{3,5},{4,2},{5,3},{6,14},{7,15},{8,0},{9,1},{10,... | collective-permute-start | bytes 884744 | tf_op jit(solution)/shard_map/ppermute | solution.py:326
  25.7 9.9 %collective-permute-start.4 = (f32[192,384]{1,0:T(8,128)S(1)}, f32[192,384]{1,0:T(8,128)S(1)}, u32[]{:S(2)}, u32[]{:S(2)}) collective-permute-start(f32[192,384]{1,0:T(8,128)S(1)} %get-tuple-element.38.green_b), channel_id=1, source_target_pairs={{0,1},{1,0},{2,3},{3,2},{4,5},{5,4},{6,7},{7,6},{8,9},{9,8},{10,11... | collective-permute-start | bytes 884744 | tf_op jit(solution)/shard_map/ppermute | solution.py:326
  27.9 13.9 %copy-start = (f32[1,384,384]{2,1,0:T(8,128)S(1)}, f32[1,384,384]{2,1,0:T(8,128)}, u32[]{:S(2)}) copy-start(f32[1,384,384]{2,1,0:T(8,128)} %param.15) | copy-start | bytes 1769476
  28.3 13.6 %collective-permute-start.11 = (f32[192,384]{1,0:T(8,128)S(1)}, f32[192,384]{1,0:T(8,128)S(1)}, u32[]{:S(2)}, u32[]{:S(2)}) collective-permute-start(f32[192,384]{1,0:T(8,128)S(1)} %get-tuple-element.44), channel_id=1, source_target_pairs={{0,1},{1,0},{2,3},{3,2},{4,5},{5,4},{6,7},{7,6},{8,9},{9,8},{10,11... | collective-permute-start | bytes 884744 | tf_op jit(solution)/shard_map/ppermute | solution.py:326
  28.6 13.6 %collective-permute-start.12 = (f32[192,384]{1,0:T(8,128)S(1)}, f32[192,384]{1,0:T(8,128)S(1)}, u32[]{:S(2)}, u32[]{:S(2)}) collective-permute-start(f32[192,384]{1,0:T(8,128)S(1)} %get-tuple-element.45), channel_id=1, source_target_pairs={{0,2},{1,3},{2,0},{3,1},{4,6},{5,7},{6,4},{7,5},{8,10},{9,11},{10,... | collective-permute-start | bytes 884744 | tf_op jit(solution)/shard_map/ppermute | solution.py:326
  34.2 8.0 %collective-permute-start.13 = (f32[192,384]{1,0:T(8,128)S(1)}, f32[192,384]{1,0:T(8,128)S(1)}, u32[]{:S(2)}, u32[]{:S(2)}) collective-permute-start(f32[192,384]{1,0:T(8,128)S(1)} %get-tuple-element.46), channel_id=1, source_target_pairs={{0,8},{1,9},{2,4},{3,5},{4,2},{5,3},{6,14},{7,15},{8,0},{9,1},{10,... | collective-permute-start | bytes 884744 | tf_op jit(solution)/shard_map/ppermute | solution.py:326
  35.9 10.9 %collective-permute-start.5 = (f32[192,384]{1,0:T(8,128)S(1)}, f32[192,384]{1,0:T(8,128)S(1)}, u32[]{:S(2)}, u32[]{:S(2)}) collective-permute-start(f32[192,384]{1,0:T(8,128)S(1)} %get-tuple-element.39), channel_id=1, source_target_pairs={{0,1},{1,0},{2,3},{3,2},{4,5},{5,4},{6,7},{7,6},{8,9},{9,8},{10,11... | collective-permute-start | bytes 884744 | tf_op jit(solution)/shard_map/ppermute | solution.py:326
  37.7 9.1 %collective-permute-start.6 = (f32[192,384]{1,0:T(8,128)S(1)}, f32[192,384]{1,0:T(8,128)S(1)}, u32[]{:S(2)}, u32[]{:S(2)}) collective-permute-start(f32[192,384]{1,0:T(8,128)S(1)} %get-tuple-element.40), channel_id=1, source_target_pairs={{0,2},{1,3},{2,0},{3,1},{4,6},{5,7},{6,4},{7,5},{8,10},{9,11},{10,... | collective-permute-start | bytes 884744 | tf_op jit(solution)/shard_map/ppermute | solution.py:326
  41.9 5.0 %collective-permute-start.7 = (f32[192,384]{1,0:T(8,128)S(1)}, f32[192,384]{1,0:T(8,128)S(1)}, u32[]{:S(2)}, u32[]{:S(2)}) collective-permute-start(f32[192,384]{1,0:T(8,128)S(1)} %get-tuple-element.41), channel_id=1, source_target_pairs={{0,8},{1,9},{2,4},{3,5},{4,2},{5,3},{6,14},{7,15},{8,0},{9,1},{10,... | collective-permute-start | bytes 884744 | tf_op jit(solution)/shard_map/ppermute | solution.py:326
